TPU v7x, 512 devices: a whole 4x4x16 slice. The times are simulated.
512 devices in a mesh: group: 8 (over y, core), box: 64 (over z, x).
Axes of the slice: x: 4, y: 4, z: 16, core: 2. Of those that a mesh axis runs over, the one named last changes fastest.
Arguments:
- dipoles: float32 [3, 131072], P(None, ('group', 'box')), may hold values from -6 to 6
- perm_field: float32 [3, 131072], P(None, ('group', 'box')), may hold values from -6 to 6
- positions: float32 [3, 131072], P(None, ('group', 'box')), may hold values from -1 to 1
- polarizability: float32 [131072], P(('group', 'box')), may hold values from 0.5 to 2.5
- occupancy: int32 [1024], P(('group', 'box')), may hold values from 1 to 128
- far_boxes: int32 [1024, 189], P(('group', 'box')), may hold values from 0 to 1023, as said below
- far_class: int32 [1024, 189], P(('group', 'box')), may hold values from 0 to 7
- far_count: int32 [1024], P(('group', 'box')), may hold values from 94 to 189
- far_scale: float32 [1024, 189], P(('group', 'box')), may hold values from 0.2 to 1
- translations: float32 [8, 165, 165], replicated, may hold values from -0.0015015624 to 0.0015015624
Outputs:
- new_dipoles: float32 [3, 131072], P(None, ('group', 'box'))
- residual: float32 [3, 131072], P(None, ('group', 'box'))
Inputs may be any that keep to these rules, and one draw needn't show every extreme that they name: Entry far_boxes[b, e] names a box of layer z' in group g' with |z' - z| <= 4 for box b's own layer z and group g, and |z' - z| >= 2 where g' = g; the first entry of every list is 4 layers away.
All inputs are finite; a program needn't handle non-finite values.
Results may differ from a plain program's by a relative error of at most 0.0003.
Values sent between devices are 32-bit elements; how exact they have to be, the bound alone decides.
No kernel may reach another device: no remote copies, remote signals or barrier semaphores. Data moves between devices by JAX's collectives and lax.ppermute only.
A program may use at most 64 MiB of HBM per device.

v0:
```python
import jax
import jax.numpy as jnp
import numpy as np
from jax import lax
from jax.sharding import PartitionSpec as P

TILE = 128
ORDER = 8
NTERM = 165
FX = 2
FY = 1
REACH = 4
CLASSES = 8


HALF = 5.4
THOLE = 0.39
SOFT = 1.0
HIGH = lax.Precision.HIGHEST


def extended(block, sides, width):
    for axis, dim in sides:
        count = lax.axis_size(axis)
        forward = [(i, i + 1) for i in range(count - 1)]
        backward = [(target, source) for source, target in forward]
        low = lax.ppermute(
            lax.slice_in_dim(block, block.shape[dim] - width, None, axis=dim), axis, forward
        )
        high = lax.ppermute(lax.slice_in_dim(block, 0, width, axis=dim), axis, backward)
        block = jnp.concatenate([low, block, high], axis=dim)
    return block


def from_behind(x, axis, by):
    peers = lax.axis_size(axis)
    pairs = [(i, i + by) for i in range(peers) if 0 <= i + by < peers]
    return lax.ppermute(x, axis, pairs)


def term_table(order):
    listing = []
    for degree in range(order + 1):
        for first_idx in range(degree + 1):
            for second_idx in range(degree + 1 - first_idx):
                listing.append((first_idx, second_idx, degree - first_idx - second_idx))
    return np.array(listing, dtype=np.int32)


def chebyshev(coord, order):
    series = [jnp.ones_like(coord), coord]
    for number in range(2, order + 1):
        series.append(2.0 * coord * series[-1] - series[-2])
    return jnp.stack(series[: order + 1])


def monomials(positions):
    table = term_table(ORDER)
    cheb_x = chebyshev(positions[0], ORDER)
    cheb_y = chebyshev(positions[1], ORDER)
    cheb_z = chebyshev(positions[2], ORDER)
    return cheb_x[table[:, 0]] * cheb_y[table[:, 1]] * cheb_z[table[:, 2]]


def pair_field(target_rel, target_root, source_rel, source_root, source_dip, offset, keep_mask):
    deltas = [
        HALF
        * (
            target_rel[component][:, :, None]
            - source_rel[component][:, None, :]
            - 2.0 * offset[component]
        )
        for component in range(3)
    ]
    squared = deltas[0] * deltas[0] + deltas[1] * deltas[1] + deltas[2] * deltas[2] + SOFT
    inverse = lax.rsqrt(squared)
    cube_inv = inverse * inverse * inverse
    strength = (
        THOLE * squared * jnp.sqrt(squared) * target_root[:, :, None] * source_root[:, None, :]
    )
    damping = jnp.exp(-strength)
    lambda_three = -jnp.expm1(-strength)
    lambda_five = lambda_three - strength * damping
    projection = (
        deltas[0] * source_dip[0][:, None, :]
        + deltas[1] * source_dip[1][:, None, :]
        + deltas[2] * source_dip[2][:, None, :]
    )
    radial = keep_mask * 3.0 * lambda_five * cube_inv * inverse * inverse * projection
    direct = keep_mask * lambda_three * cube_inv
    return jnp.stack(
        [
            jnp.sum(deltas[component] * radial - direct * source_dip[component][:, None, :], axis=2)
            for component in range(3)
        ]
    )


def near_operator(dipole_src, geometry, target_rel, target_root):
    box_dev = FX * FY
    shaped = dipole_src.reshape(3, 1, FX, FY, TILE)
    layers = extended(shaped, (("box", 1),), 1)
    padded = jnp.pad(layers, ((0, 0), (0, 0), (1, 1), (1, 1), (0, 0)))
    total = jnp.zeros((3, box_dev, TILE), jnp.float32)
    for shift_z in (-1, 0, 1):
        for shift_x in (-1, 0, 1):
            for shift_y in (-1, 0, 1):
                window_dip = padded[
                    :, 1 + shift_z, 1 + shift_x : 1 + shift_x + FX, 1 + shift_y : 1 + shift_y + FY
                ].reshape(3, box_dev, TILE)
                window_geo = geometry[
                    :, 1 + shift_z, 1 + shift_x : 1 + shift_x + FX, 1 + shift_y : 1 + shift_y + FY
                ].reshape(4, box_dev, TILE)
                if shift_z == 0 and shift_x == 0 and (shift_y == 0):
                    keep_mask = 1.0 - jnp.eye(TILE, dtype=jnp.float32)
                else:
                    keep_mask = jnp.float32(1.0)
                total = total + pair_field(
                    target_rel,
                    target_root,
                    window_geo[:3],
                    window_geo[3],
                    window_dip,
                    (float(shift_x), float(shift_y), float(shift_z)),
                    keep_mask,
                )
    return total.reshape(3, -1)


def far_field(source, monomial, far_boxes, far_class, far_count, far_scale, translations):
    box_dev = far_boxes.shape[0]
    mono_b = monomial.reshape(NTERM, box_dev, TILE)
    dip_b = source.reshape(3, box_dev, TILE)
    multipole = jnp.einsum("tbs,cbs->bct", mono_b, dip_b, precision=HIGH).reshape(
        box_dev, 3 * NTERM
    )
    groups = lax.axis_size("group")
    owners = lax.axis_size("box")
    layer = lax.axis_index("box")
    device = far_boxes // box_dev
    stride = device % owners - layer + REACH
    other = device // owners
    within = far_boxes % box_dev
    pieces = []
    gathered = lax.all_gather(multipole[None], "group", axis=0, tiled=True)
    for offset in range(-REACH, REACH + 1):
        if offset == 0:
            pieces.append(gathered)
        else:
            pieces.append(from_behind(gathered, "box", -offset))
    window = jnp.stack(pieces)
    location = (stride * groups + other) * box_dev + within
    flat = window.reshape(-1, 3 * NTERM)
    listing = lax.broadcasted_iota(jnp.int32, far_boxes.shape, 1)
    weights = far_scale * (listing < far_count[:, None]).astype(jnp.float32)
    classes = (far_class[:, :, None] == lax.broadcasted_iota(jnp.int32, (1, 1, CLASSES), 2)).astype(
        jnp.float32
    ) * weights[:, :, None]
    matches = (
        location[:, :, None] == lax.broadcasted_iota(jnp.int32, (1, 1, flat.shape[0]), 2)
    ).astype(jnp.float32)
    selector = jnp.einsum("kjo,kjn->kon", classes, matches, precision=HIGH)
    summed = jnp.einsum("kon,nq->koq", selector, flat, precision=HIGH).reshape(
        box_dev, CLASSES, 3, NTERM
    )
    local = jnp.einsum("kocu,otu->kct", summed, translations, precision=HIGH)
    return jnp.einsum("tks,kct->cks", mono_b, local, precision=HIGH).reshape(3, -1)


def on_device(
    dipoles,
    perm_field,
    positions,
    polarizability,
    occupancy,
    far_boxes,
    far_class,
    far_count,
    far_scale,
    translations,
):
    box_dev = occupancy.shape[0]
    slot = lax.broadcasted_iota(jnp.int32, (box_dev, TILE), 1)
    live_mask = (slot < occupancy[:, None]).astype(jnp.float32).reshape(-1)
    source = dipoles * live_mask
    root_pol = lax.rsqrt(polarizability)
    geometry = jnp.concatenate([positions, root_pol[None]], axis=0).reshape(4, 1, FX, FY, TILE)
    neighbours = extended(geometry, (("box", 1),), 1)
    neighbours = jnp.pad(neighbours, ((0, 0), (0, 0), (1, 1), (1, 1), (0, 0)))
    target_rel = positions.reshape(3, box_dev, TILE)
    target_root = root_pol.reshape(box_dev, TILE)
    monomial = monomials(positions)
    far_part = far_field(source, monomial, far_boxes, far_class, far_count, far_scale, translations)
    near_zero = near_operator(source, neighbours, target_rel, target_root)
    residual = live_mask * (perm_field + far_part + near_zero - source / polarizability)
    sweep_one = polarizability * residual
    sweep_two = (
        live_mask
        * polarizability
        * (residual + near_operator(sweep_one, neighbours, target_rel, target_root))
    )
    sweep_three = (
        live_mask
        * polarizability
        * (residual + near_operator(sweep_two, neighbours, target_rel, target_root))
    )
    return (source + sweep_three, residual)


def solution(mesh):
    return jax.shard_map(
        on_device,
        mesh=mesh,
        in_specs=(
            P(None, ("group", "box")),
            P(None, ("group", "box")),
            P(None, ("group", "box")),
            P(("group", "box")),
            P(("group", "box")),
            P(("group", "box"), None),
            P(("group", "box"), None),
            P(("group", "box")),
            P(("group", "box"), None),
            P(),
        ),
        out_specs=(P(None, ("group", "box")), P(None, ("group", "box"))),
        check_vma=False,
    )
```

profile of v0, /device:TPU:102, one launch (start us, length us, event | category | flops | bytes accessed | tf_op | source)
XLA Modules:
  0.0 118.2 jit_solution(14500830830824224616)
XLA Ops:
  0.6 0.7 bitcast_convert_fusion
  1.4 0.7 bitcast_select_fusion
  2.1 0.9 subtract_multiply_fusion.86
  3.0 0.9 subtract_multiply_fusion.89
  3.8 0.9 subtract_multiply_fusion.104
  4.7 0.7 pad_clamp_fusion.2
  5.4 0.9 subtract_multiply_fusion.107
  6.3 0.7 pad_clamp_fusion
  7.0 0.8 subtract_multiply_fusion.112
  7.8 0.8 subtract_multiply_fusion.109
  8.7 0.8 gather_fusion.1
  9.6 0.8 gather_fusion
  10.5 0.8 gather_fusion.2
  11.9 13.4 %all_gather.3 = f32[8,2,495]{2,1,0:T(2,128)S(1)} all-gather(f32[1,2,495]{2,1,0:T(2,128)S(1)} %broadcast_in_dim_reshape.2), channel_id=1, replica_groups=mesh['group'=8,'box'=64] {'group'}, dimensions={0}, use_global_device_ids=true | all-gather | bytes 35640 | tf_op jit(solution)/shard_map/all_gather | solution.py:145
  25.4 5.0 %collective-permute-start = (f32[8,2,495]{2,1,0:T(2,128)S(1)}, f32[8,2,495]{2,1,0:T(2,128)S(1)}, u32[]{:S(2)}, u32[]{:S(2)}) collective-permute-start(f32[8,2,495]{2,1,0:T(2,128)S(1)} %all_gather.3), channel_id=1, source_target_pairs={{0,4},{1,5},{2,6},{3,7},{4,8},{5,9},{6,10},{7,11},{8,12},{9,13},{1... | collective-permute-start | bytes 95048 | tf_op jit(solution)/shard_map/ppermute | solution.py:38
  30.4 4.1 %collective-permute-start.1 = (f32[8,2,495]{2,1,0:T(2,128)S(1)}, f32[8,2,495]{2,1,0:T(2,128)S(1)}, u32[]{:S(2)}, u32[]{:S(2)}) collective-permute-start(f32[8,2,495]{2,1,0:T(2,128)S(1)} %all_gather.3), channel_id=1, source_target_pairs={{0,3},{1,4},{2,5},{3,6},{4,7},{5,8},{6,9},{7,10},{8,11},{9,12},{10... | collective-permute-start | bytes 95048 | tf_op jit(solution)/shard_map/ppermute | solution.py:38
  34.5 4.4 %collective-permute-start.2 = (f32[8,2,495]{2,1,0:T(2,128)S(1)}, f32[8,2,495]{2,1,0:T(2,128)S(1)}, u32[]{:S(2)}, u32[]{:S(2)}) collective-permute-start(f32[8,2,495]{2,1,0:T(2,128)S(1)} %all_gather.3), channel_id=1, source_target_pairs={{0,2},{1,3},{2,4},{3,5},{4,6},{5,7},{6,8},{7,9},{8,10},{9,11},{10,... | collective-permute-start | bytes 95048 | tf_op jit(solution)/shard_map/ppermute | solution.py:38
  38.9 4.0 %collective-permute-start.10 = (f32[3,1,2,1,128]{4,2,3,1,0:T(2,128)S(1)}, f32[3,1,2,1,128]{4,2,3,1,0:T(2,128)S(1)}, u32[]{:S(2)}, u32[]{:S(2)}) collective-permute-start(f32[3,1,2,1,128]{4,2,3,1,0:T(2,128)S(1)} %bitcast.520), channel_id=1, source_target_pairs={{0,1},{1,2},{2,3},{3,4},{4,5},{5,6},{6,7},{7,8},{8,9},{9,10},{10,1... | collective-permute-start | bytes 9224 | tf_op jit(solution)/shard_map/ppermute | solution.py:27
  42.9 1.9 %collective-permute-start.11 = (f32[3,1,2,1,128]{4,2,3,1,0:T(2,128)S(1)}, f32[3,1,2,1,128]{4,2,3,1,0:T(2,128)S(1)}, u32[]{:S(2)}, u32[]{:S(2)}) collective-permute-start(f32[3,1,2,1,128]{4,2,3,1,0:T(2,128)S(1)} %bitcast.521), channel_id=1, source_target_pairs={{1,0},{2,1},{3,2},{4,3},{5,4},{6,5},{7,6},{8,7},{9,8},{10,9},{11,1... | collective-permute-start | bytes 9224 | tf_op jit(solution)/shard_map/ppermute | solution.py:30
  45.4 0.5 fusion.141
  45.9 7.2 %collective-permute-start.8 = (f32[4,1,2,1,128]{4,2,0,3,1:T(2,128)S(1)}, f32[4,1,2,1,128]{4,2,0,3,1:T(2,128)S(1)}, u32[]{:S(2)}, u32[]{:S(2)}) collective-permute-start(f32[4,1,2,1,128]{4,2,0,3,1:T(2,128)S(1)} %pad_maximum_fusion.1), channel_id=1, source_target_pairs={{0,1},{1,2},{2,3},{3,4},{4,5},{5,6},{6,7},{7,8},{8,9},{9,10},{10,1... | collective-permute-start | bytes 12296 | tf_op jit(solution)/shard_map/ppermute | solution.py:27
  53.2 1.9 %collective-permute-start.9 = (f32[4,1,2,1,128]{4,2,0,3,1:T(2,128)S(1)}, f32[4,1,2,1,128]{4,2,0,3,1:T(2,128)S(1)}, u32[]{:S(2)}, u32[]{:S(2)}) collective-permute-start(f32[4,1,2,1,128]{4,2,0,3,1:T(2,128)S(1)} %pad_maximum_fusion.1), channel_id=1, source_target_pairs={{1,0},{2,1},{3,2},{4,3},{5,4},{6,5},{7,6},{8,7},{9,8},{10,9},{11,1... | collective-permute-start | bytes 12296 | tf_op jit(solution)/shard_map/ppermute | solution.py:30
  55.2 7.2 %collective-permute-start.3 = (f32[8,2,495]{2,1,0:T(2,128)S(1)}, f32[8,2,495]{2,1,0:T(2,128)S(1)}, u32[]{:S(2)}, u32[]{:S(2)}) collective-permute-start(f32[8,2,495]{2,1,0:T(2,128)S(1)} %all_gather.3), channel_id=1, source_target_pairs={{0,1},{1,2},{2,3},{3,4},{4,5},{5,6},{6,7},{7,8},{8,9},{9,10},{10,1... | collective-permute-start | bytes 95048 | tf_op jit(solution)/shard_map/ppermute | solution.py:38
  62.5 1.9 %collective-permute-start.4 = (f32[8,2,495]{2,1,0:T(2,128)S(1)}, f32[8,2,495]{2,1,0:T(2,128)S(1)}, u32[]{:S(2)}, u32[]{:S(2)}) collective-permute-start(f32[8,2,495]{2,1,0:T(2,128)S(1)} %all_gather.3), channel_id=1, source_target_pairs={{1,0},{2,1},{3,2},{4,3},{5,4},{6,5},{7,6},{8,7},{9,8},{10,9},{11,1... | collective-permute-start | bytes 95048 | tf_op jit(solution)/shard_map/ppermute | solution.py:38
  64.5 0.5 subtract_reduce_fusion.35
  65.0 0.5 fusion.180
  65.6 0.5 subtract_reduce_fusion.32
  66.1 0.5 subtract_reduce_fusion.30
  66.6 0.5 subtract_reduce_fusion.29
  67.2 0.5 subtract_reduce_fusion.28
  67.7 0.5 fusion.96
  68.2 0.5 subtract_reduce_fusion.25
  68.8 1.9 %collective-permute-start.5 = (f32[8,2,495]{2,1,0:T(2,128)S(1)}, f32[8,2,495]{2,1,0:T(2,128)S(1)}, u32[]{:S(2)}, u32[]{:S(2)}) collective-permute-start(f32[8,2,495]{2,1,0:T(2,128)S(1)} %all_gather.3), channel_id=1, source_target_pairs={{2,0},{3,1},{4,2},{5,3},{6,4},{7,5},{8,6},{9,7},{10,8},{11,9},{12,... | collective-permute-start | bytes 95048 | tf_op jit(solution)/shard_map/ppermute | solution.py:38
  70.7 2.3 %collective-permute-start.6 = (f32[8,2,495]{2,1,0:T(2,128)S(1)}, f32[8,2,495]{2,1,0:T(2,128)S(1)}, u32[]{:S(2)}, u32[]{:S(2)}) collective-permute-start(f32[8,2,495]{2,1,0:T(2,128)S(1)} %all_gather.3), channel_id=1, source_target_pairs={{3,0},{4,1},{5,2},{6,3},{7,4},{8,5},{9,6},{10,7},{11,8},{12,9},{13... | collective-permute-start | bytes 95048 | tf_op jit(solution)/shard_map/ppermute | solution.py:38
  73.0 2.0 %collective-permute-start.7 = (f32[8,2,495]{2,1,0:T(2,128)S(1)}, f32[8,2,495]{2,1,0:T(2,128)S(1)}, u32[]{:S(2)}, u32[]{:S(2)}) collective-permute-start(f32[8,2,495]{2,1,0:T(2,128)S(1)} %all_gather.3), channel_id=1, source_target_pairs={{4,0},{5,1},{6,2},{7,3},{8,4},{9,5},{10,6},{11,7},{12,8},{13,9},{1... | collective-permute-start | bytes 95048 | tf_op jit(solution)/shard_map/ppermute | solution.py:38
  75.1 3.1 %collective-permute-done.5 = f32[8,2,495]{2,1,0:T(2,128)S(1)} collective-permute-done((f32[8,2,495]{2,1,0:T(2,128)S(1)}, f32[8,2,495]{2,1,0:T(2,128)S(1)}, u32[]{:S(2)}, u32[]{:S(2)}) %collective-permute-start.5) | collective-permute-done | bytes 31712 | tf_op jit(solution)/shard_map/ppermute | solution.py:38
  78.2 2.5 %collective-permute-done.6 = f32[8,2,495]{2,1,0:T(2,128)S(1)} collective-permute-done((f32[8,2,495]{2,1,0:T(2,128)S(1)}, f32[8,2,495]{2,1,0:T(2,128)S(1)}, u32[]{:S(2)}, u32[]{:S(2)}) %collective-permute-start.6) | collective-permute-done | bytes 31712 | tf_op jit(solution)/shard_map/ppermute | solution.py:38
  80.7 1.7 %collective-permute-done.7 = f32[8,2,495]{2,1,0:T(2,128)S(1)} collective-permute-done((f32[8,2,495]{2,1,0:T(2,128)S(1)}, f32[8,2,495]{2,1,0:T(2,128)S(1)}, u32[]{:S(2)}, u32[]{:S(2)}) %collective-permute-start.7) | collective-permute-done | bytes 31712 | tf_op jit(solution)/shard_map/ppermute | solution.py:38
  83.3 1.6 %fusion.3 = f32[2,3,165]{2,1,0:T(4,128)S(1)} fusion(f32[8,165,165]{2,0,1:T(8,128)S(1)} %copy-done, f32[2,8,3,165]{3,1,2,0:T(8,128)S(1)} %fusion.10), kind=kOutput, calls=%fused_computation.7 | convolution fusion | flops 15681600 | bytes 906840 | tf_op jit(solution)/shard_map/kocu,otu->kct/dot_general | solution.py:166
  85.3 3.7 %collective-permute-start.12 = (f32[3,1,2,1,128]{4,2,3,1,0:T(2,128)S(1)}, f32[3,1,2,1,128]{4,2,3,1,0:T(2,128)S(1)}, u32[]{:S(2)}, u32[]{:S(2)}) collective-permute-start(f32[3,1,2,1,128]{4,2,3,1,0:T(2,128)S(1)} %bitcast.526), channel_id=1, source_target_pairs={{0,1},{1,2},{2,3},{3,4},{4,5},{5,6},{6,7},{7,8},{8,9},{9,10},{10,1... | collective-permute-start | bytes 9224 | tf_op jit(solution)/shard_map/ppermute | solution.py:27
  89.0 2.4 %collective-permute-start.13 = (f32[3,1,2,1,128]{4,2,3,1,0:T(2,128)S(1)}, f32[3,1,2,1,128]{4,2,3,1,0:T(2,128)S(1)}, u32[]{:S(2)}, u32[]{:S(2)}) collective-permute-start(f32[3,1,2,1,128]{4,2,3,1,0:T(2,128)S(1)} %bitcast.527), channel_id=1, source_target_pairs={{1,0},{2,1},{3,2},{4,3},{5,4},{6,5},{7,6},{8,7},{9,8},{10,9},{11,1... | collective-permute-start | bytes 9224 | tf_op jit(solution)/shard_map/ppermute | solution.py:30
  91.4 0.5 fusion.143
  91.9 5.9 %collective-permute-done.13 = f32[3,1,2,1,128]{4,2,3,1,0:T(2,128)S(1)} collective-permute-done((f32[3,1,2,1,128]{4,2,3,1,0:T(2,128)S(1)}, f32[3,1,2,1,128]{4,2,3,1,0:T(2,128)S(1)}, u32[]{:S(2)}, u32[]{:S(2)}) %collective-permute-start.13) | collective-permute-done | bytes 3104 | tf_op jit(solution)/shard_map/ppermute | solution.py:30
  97.9 0.5 subtract_reduce_fusion.23
  98.4 0.5 fusion.182
  99.0 0.5 subtract_reduce_fusion.20
  99.5 0.5 subtract_reduce_fusion.18
  100.0 0.5 subtract_reduce_fusion.17
  100.5 0.5 subtract_reduce_fusion.16
  101.1 0.5 fusion.98
  101.6 0.5 subtract_reduce_fusion.13
  102.3 1.9 %collective-permute-start.14 = (f32[3,1,2,1,128]{4,2,3,1,0:T(2,128)S(1)}, f32[3,1,2,1,128]{4,2,3,1,0:T(2,128)S(1)}, u32[]{:S(2)}, u32[]{:S(2)}) collective-permute-start(f32[3,1,2,1,128]{4,2,3,1,0:T(2,128)S(1)} %bitcast.523), channel_id=1, source_target_pairs={{0,1},{1,2},{2,3},{3,4},{4,5},{5,6},{6,7},{7,8},{8,9},{9,10},{10,1... | collective-permute-start | bytes 9224 | tf_op jit(solution)/shard_map/ppermute | solution.py:27
  104.2 3.9 %collective-permute-start.15 = (f32[3,1,2,1,128]{4,2,3,1,0:T(2,128)S(1)}, f32[3,1,2,1,128]{4,2,3,1,0:T(2,128)S(1)}, u32[]{:S(2)}, u32[]{:S(2)}) collective-permute-start(f32[3,1,2,1,128]{4,2,3,1,0:T(2,128)S(1)} %bitcast.524), channel_id=1, source_target_pairs={{1,0},{2,1},{3,2},{4,3},{5,4},{6,5},{7,6},{8,7},{9,8},{10,9},{11,1... | collective-permute-start | bytes 9224 | tf_op jit(solution)/shard_map/ppermute | solution.py:30
  108.2 0.5 fusion.145
  108.7 4.3 %collective-permute-done.15 = f32[3,1,2,1,128]{4,2,3,1,0:T(2,128)S(1)} collective-permute-done((f32[3,1,2,1,128]{4,2,3,1,0:T(2,128)S(1)}, f32[3,1,2,1,128]{4,2,3,1,0:T(2,128)S(1)}, u32[]{:S(2)}, u32[]{:S(2)}) %collective-permute-start.15) | collective-permute-done | bytes 3104 | tf_op jit(solution)/shard_map/ppermute | solution.py:30
  113.1 0.5 subtract_reduce_fusion.11
  113.7 0.5 fusion.184
  114.2 0.5 subtract_reduce_fusion.8
  114.7 0.5 subtract_reduce_fusion.6
  115.3 0.5 subtract_reduce_fusion.5
  115.8 0.5 subtract_reduce_fusion.4
  116.3 0.5 fusion.100
  116.9 0.5 subtract_reduce_fusion.1
  117.4 0.8 multiply_add_fusion
  (104 shorter events, 3.1 us)
Async XLA Ops:
  10.4 1.1 copy-start.3
  10.4 34.4 %copy-start.1 = (f32[3,256]{1,0:T(4,128)S(1)}, f32[3,256]{1,0:T(4,128)}, u32[]{:S(2)}) copy-start(f32[3,256]{1,0:T(4,128)} %param.18) | copy-start | bytes 9220
  10.4 34.5 %copy-start.4 = (s32[2,189]{1,0:T(2,128)S(1)}, s32[2,189]{1,0:T(2,128)}, u32[]{:S(2)}) copy-start(s32[2,189]{1,0:T(2,128)} %param.21) | copy-start | bytes 4540
  10.5 34.5 %copy-start.5 = (f32[2,189]{1,0:T(2,128)S(1)}, f32[2,189]{1,0:T(2,128)}, u32[]{:S(2)}) copy-start(f32[2,189]{1,0:T(2,128)} %param.24) | copy-start | bytes 4540
  10.5 34.5 %copy-start.7 = (s32[2]{0:T(128)S(1)}, s32[2]{0:T(128)}, u32[]{:S(2)}) copy-start(s32[2]{0:T(128)} %param.23) | copy-start | bytes 28
  10.5 34.6 %copy-start.9 = (s32[2,189]{1,0:T(2,128)S(1)}, s32[2,189]{1,0:T(2,128)}, u32[]{:S(2)}) copy-start(s32[2,189]{1,0:T(2,128)} %param.22) | copy-start | bytes 4540
  25.4 43.4 %collective-permute-start = (f32[8,2,495]{2,1,0:T(2,128)S(1)}, f32[8,2,495]{2,1,0:T(2,128)S(1)}, u32[]{:S(2)}, u32[]{:S(2)}) collective-permute-start(f32[8,2,495]{2,1,0:T(2,128)S(1)} %all_gather.3), channel_id=1, source_target_pairs={{0,4},{1,5},{2,6},{3,7},{4,8},{5,9},{6,10},{7,11},{8,12},{9,13},{1... | collective-permute-start | bytes 95048 | tf_op jit(solution)/shard_map/ppermute | solution.py:38
  30.4 40.3 %collective-permute-start.1 = (f32[8,2,495]{2,1,0:T(2,128)S(1)}, f32[8,2,495]{2,1,0:T(2,128)S(1)}, u32[]{:S(2)}, u32[]{:S(2)}) collective-permute-start(f32[8,2,495]{2,1,0:T(2,128)S(1)} %all_gather.3), channel_id=1, source_target_pairs={{0,3},{1,4},{2,5},{3,6},{4,7},{5,8},{6,9},{7,10},{8,11},{9,12},{10... | collective-permute-start | bytes 95048 | tf_op jit(solution)/shard_map/ppermute | solution.py:38
  34.5 38.5 %collective-permute-start.2 = (f32[8,2,495]{2,1,0:T(2,128)S(1)}, f32[8,2,495]{2,1,0:T(2,128)S(1)}, u32[]{:S(2)}, u32[]{:S(2)}) collective-permute-start(f32[8,2,495]{2,1,0:T(2,128)S(1)} %all_gather.3), channel_id=1, source_target_pairs={{0,2},{1,3},{2,4},{3,5},{4,6},{5,7},{6,8},{7,9},{8,10},{9,11},{10,... | collective-permute-start | bytes 95048 | tf_op jit(solution)/shard_map/ppermute | solution.py:38
  38.9 7.0 %collective-permute-start.10 = (f32[3,1,2,1,128]{4,2,3,1,0:T(2,128)S(1)}, f32[3,1,2,1,128]{4,2,3,1,0:T(2,128)S(1)}, u32[]{:S(2)}, u32[]{:S(2)}) collective-permute-start(f32[3,1,2,1,128]{4,2,3,1,0:T(2,128)S(1)} %bitcast.520), channel_id=1, source_target_pairs={{0,1},{1,2},{2,3},{3,4},{4,5},{5,6},{6,7},{7,8},{8,9},{9,10},{10,1... | collective-permute-start | bytes 9224 | tf_op jit(solution)/shard_map/ppermute | solution.py:27
  42.9 10.3 %collective-permute-start.11 = (f32[3,1,2,1,128]{4,2,3,1,0:T(2,128)S(1)}, f32[3,1,2,1,128]{4,2,3,1,0:T(2,128)S(1)}, u32[]{:S(2)}, u32[]{:S(2)}) collective-permute-start(f32[3,1,2,1,128]{4,2,3,1,0:T(2,128)S(1)} %bitcast.521), channel_id=1, source_target_pairs={{1,0},{2,1},{3,2},{4,3},{5,4},{6,5},{7,6},{8,7},{9,8},{10,9},{11,1... | collective-permute-start | bytes 9224 | tf_op jit(solution)/shard_map/ppermute | solution.py:30
  45.9 9.3 %collective-permute-start.8 = (f32[4,1,2,1,128]{4,2,0,3,1:T(2,128)S(1)}, f32[4,1,2,1,128]{4,2,0,3,1:T(2,128)S(1)}, u32[]{:S(2)}, u32[]{:S(2)}) collective-permute-start(f32[4,1,2,1,128]{4,2,0,3,1:T(2,128)S(1)} %pad_maximum_fusion.1), channel_id=1, source_target_pairs={{0,1},{1,2},{2,3},{3,4},{4,5},{5,6},{6,7},{7,8},{8,9},{9,10},{10,1... | collective-permute-start | bytes 12296 | tf_op jit(solution)/shard_map/ppermute | solution.py:27
  53.2 9.3 %collective-permute-start.9 = (f32[4,1,2,1,128]{4,2,0,3,1:T(2,128)S(1)}, f32[4,1,2,1,128]{4,2,0,3,1:T(2,128)S(1)}, u32[]{:S(2)}, u32[]{:S(2)}) collective-permute-start(f32[4,1,2,1,128]{4,2,0,3,1:T(2,128)S(1)} %pad_maximum_fusion.1), channel_id=1, source_target_pairs={{1,0},{2,1},{3,2},{4,3},{5,4},{6,5},{7,6},{8,7},{9,8},{10,9},{11,1... | collective-permute-start | bytes 12296 | tf_op jit(solution)/shard_map/ppermute | solution.py:30
  55.2 19.8 %collective-permute-start.3 = (f32[8,2,495]{2,1,0:T(2,128)S(1)}, f32[8,2,495]{2,1,0:T(2,128)S(1)}, u32[]{:S(2)}, u32[]{:S(2)}) collective-permute-start(f32[8,2,495]{2,1,0:T(2,128)S(1)} %all_gather.3), channel_id=1, source_target_pairs={{0,1},{1,2},{2,3},{3,4},{4,5},{5,6},{6,7},{7,8},{8,9},{9,10},{10,1... | collective-permute-start | bytes 95048 | tf_op jit(solution)/shard_map/ppermute | solution.py:38
  62.5 12.6 %collective-permute-start.4 = (f32[8,2,495]{2,1,0:T(2,128)S(1)}, f32[8,2,495]{2,1,0:T(2,128)S(1)}, u32[]{:S(2)}, u32[]{:S(2)}) collective-permute-start(f32[8,2,495]{2,1,0:T(2,128)S(1)} %all_gather.3), channel_id=1, source_target_pairs={{1,0},{2,1},{3,2},{4,3},{5,4},{6,5},{7,6},{8,7},{9,8},{10,9},{11,1... | collective-permute-start | bytes 95048 | tf_op jit(solution)/shard_map/ppermute | solution.py:38
  68.2 15.1 %copy-start = (f32[8,165,165]{2,0,1:T(8,128)S(1)}, f32[8,165,165]{2,0,1:T(8,128)}, u32[]{:S(2)}) copy-start(f32[8,165,165]{2,0,1:T(8,128)} %param.25) | copy-start | bytes 2613604
  68.8 9.4 %collective-permute-start.5 = (f32[8,2,495]{2,1,0:T(2,128)S(1)}, f32[8,2,495]{2,1,0:T(2,128)S(1)}, u32[]{:S(2)}, u32[]{:S(2)}) collective-permute-start(f32[8,2,495]{2,1,0:T(2,128)S(1)} %all_gather.3), channel_id=1, source_target_pairs={{2,0},{3,1},{4,2},{5,3},{6,4},{7,5},{8,6},{9,7},{10,8},{11,9},{12,... | collective-permute-start | bytes 95048 | tf_op jit(solution)/shard_map/ppermute | solution.py:38
  70.7 10.0 %collective-permute-start.6 = (f32[8,2,495]{2,1,0:T(2,128)S(1)}, f32[8,2,495]{2,1,0:T(2,128)S(1)}, u32[]{:S(2)}, u32[]{:S(2)}) collective-permute-start(f32[8,2,495]{2,1,0:T(2,128)S(1)} %all_gather.3), channel_id=1, source_target_pairs={{3,0},{4,1},{5,2},{6,3},{7,4},{8,5},{9,6},{10,7},{11,8},{12,9},{13... | collective-permute-start | bytes 95048 | tf_op jit(solution)/shard_map/ppermute | solution.py:38
  73.0 9.3 %collective-permute-start.7 = (f32[8,2,495]{2,1,0:T(2,128)S(1)}, f32[8,2,495]{2,1,0:T(2,128)S(1)}, u32[]{:S(2)}, u32[]{:S(2)}) collective-permute-start(f32[8,2,495]{2,1,0:T(2,128)S(1)} %all_gather.3), channel_id=1, source_target_pairs={{4,0},{5,1},{6,2},{7,3},{8,4},{9,5},{10,6},{11,7},{12,8},{13,9},{1... | collective-permute-start | bytes 95048 | tf_op jit(solution)/shard_map/ppermute | solution.py:38
  82.6 2.4 %copy-start.6 = (f32[256]{0:T(256)S(1)}, f32[256]{0:T(256)}, u32[]{:S(2)}) copy-start(f32[256]{0:T(256)} %param.19) | copy-start | bytes 3076
  82.6 2.4 %copy-start.8 = (f32[3,256]{1,0:T(4,128)S(1)}, f32[3,256]{1,0:T(4,128)}, u32[]{:S(2)}) copy-start(f32[3,256]{1,0:T(4,128)} %param.17) | copy-start | bytes 9220
  85.3 32.1 %copy-start.2 = (f32[3,256]{1,0:T(4,128)}, f32[3,256]{1,0:T(4,128)S(1)}, u32[]{:S(2)}) copy-start(f32[3,256]{1,0:T(4,128)S(1)} %get-tuple-element.488) | copy-start | bytes 9220
  85.3 6.6 %collective-permute-start.12 = (f32[3,1,2,1,128]{4,2,3,1,0:T(2,128)S(1)}, f32[3,1,2,1,128]{4,2,3,1,0:T(2,128)S(1)}, u32[]{:S(2)}, u32[]{:S(2)}) collective-permute-start(f32[3,1,2,1,128]{4,2,3,1,0:T(2,128)S(1)} %bitcast.526), channel_id=1, source_target_pairs={{0,1},{1,2},{2,3},{3,4},{4,5},{5,6},{6,7},{7,8},{8,9},{9,10},{10,1... | collective-permute-start | bytes 9224 | tf_op jit(solution)/shard_map/ppermute | solution.py:27
  89.0 8.8 %collective-permute-start.13 = (f32[3,1,2,1,128]{4,2,3,1,0:T(2,128)S(1)}, f32[3,1,2,1,128]{4,2,3,1,0:T(2,128)S(1)}, u32[]{:S(2)}, u32[]{:S(2)}) collective-permute-start(f32[3,1,2,1,128]{4,2,3,1,0:T(2,128)S(1)} %bitcast.527), channel_id=1, source_target_pairs={{1,0},{2,1},{3,2},{4,3},{5,4},{6,5},{7,6},{8,7},{9,8},{10,9},{11,1... | collective-permute-start | bytes 9224 | tf_op jit(solution)/shard_map/ppermute | solution.py:30
  102.3 6.4 %collective-permute-start.14 = (f32[3,1,2,1,128]{4,2,3,1,0:T(2,128)S(1)}, f32[3,1,2,1,128]{4,2,3,1,0:T(2,128)S(1)}, u32[]{:S(2)}, u32[]{:S(2)}) collective-permute-start(f32[3,1,2,1,128]{4,2,3,1,0:T(2,128)S(1)} %bitcast.523), channel_id=1, source_target_pairs={{0,1},{1,2},{2,3},{3,4},{4,5},{5,6},{6,7},{7,8},{8,9},{9,10},{10,1... | collective-permute-start | bytes 9224 | tf_op jit(solution)/shard_map/ppermute | solution.py:27
  104.2 8.8 %collective-permute-start.15 = (f32[3,1,2,1,128]{4,2,3,1,0:T(2,128)S(1)}, f32[3,1,2,1,128]{4,2,3,1,0:T(2,128)S(1)}, u32[]{:S(2)}, u32[]{:S(2)}) collective-permute-start(f32[3,1,2,1,128]{4,2,3,1,0:T(2,128)S(1)} %bitcast.524), channel_id=1, source_target_pairs={{1,0},{2,1},{3,2},{4,3},{5,4},{6,5},{7,6},{8,7},{9,8},{10,9},{11,1... | collective-permute-start | bytes 9224 | tf_op jit(solution)/shard_map/ppermute | solution.py:30
where the time goes:
time: 119 us; the launch traced here: 118 us
  starting transfers between devices  55.8 us (47%)
  other arithmetic  23.6 us (20%)
  waiting for transfers between devices  17.4 us (15%)
  blocking collectives  13.4 us (11%)
  local copies, waits for them, and re-layouts  3.65 us (3%)
  matrix products  2.88 us (2%)
  between operations  1.44 us (1%)
    ppermute x8, starting transfers between devices, from_behind(): return lax.ppermute(x, axis, pairs)  28.8 us
    reduce_sum x37, other arithmetic, pair_field(): jnp.sum(deltas[component] * radial - direct * source_dip[component][:, No...  19.4 us
    ppermute x4, starting transfers between devices, extended(): lax.ppermute(lax.slice_in_dim(block, block.shape[dim] - width, None, axis...  16.8 us
    all_gather x1, blocking collectives, far_field(): gathered = lax.all_gather(multipole[None], 'group', axis=0, tiled=True)  13.4 us
    ppermute x4, waiting for transfers between devices, extended(): lax.ppermute(lax.slice_in_dim(block, 0, width, axis=dim), axis, backward)  10.2 us
    ppermute x4, starting transfers between devices, extended(): lax.ppermute(lax.slice_in_dim(block, 0, width, axis=dim), axis, backward)  10.1 us
    ppermute x8, waiting for transfers between devices, from_behind(): return lax.ppermute(x, axis, pairs)  7.23 us
    gather x3, local copies, waits for them, and re-layouts, monomials(): return cheb_x[table[:, 0]] * cheb_y[table[:, 1]] * cheb_z[table[:, 2]]  2.47 us
  transfers between devices with their start and end apart: 16, of which 5 were waited for; matrix products, arithmetic and copies ran while one was open for 5% of the time, Pallas kernels for 0%

commit v1 on v0

v1 whole, which is shorter than its diff:
```python
import jax
import jax.numpy as jnp
import numpy as np
from jax import lax
from jax.experimental import pallas as pl
from jax.experimental.pallas import tpu as pltpu
from jax.sharding import Mesh
from jax.sharding import PartitionSpec as P

TILE = 128
ORDER = 8
NTERM = 165
REST = NTERM - TILE
ILIST = 189
CLASSES = 8
GROUPS = 8
OWNERS = 64
NX = 4
NY = 4
PLANE = NX * NY
CHUNK = 48
F32 = jnp.float32
BF16 = jnp.bfloat16

HALF = 5.4
ROOT_THOLE = 0.39**0.5
HIGH = lax.Precision.HIGHEST
NT = (((1,), (1,)), ((), ()))
NN = (((1,), (0,)), ((), ()))


def term_table():
    listing = []
    for degree in range(ORDER + 1):
        for first in range(degree + 1):
            for second in range(degree + 1 - first):
                listing.append((first, second, degree - first - second))
    return listing


TERMS = term_table()


def dot(a, b, dims, precision=HIGH):
    return lax.dot_general(a, b, dims, precision=precision, preferred_element_type=F32)


def chebyshev(coord):
    series = [None, coord]
    doubled = 2.0 * coord
    series.append(doubled * coord - 1.0)
    for _ in range(3, ORDER + 1):
        series.append(doubled * series[-1] - series[-2])
    return series


def write_monomials(ref, px, py, pz):
    cx, cy, cz = chebyshev(px), chebyshev(py), chebyshev(pz)
    cross = {}
    for t, (i, j, k) in enumerate(TERMS):
        if (i, j) not in cross:
            if i and j:
                cross[i, j] = cx[i] * cy[j]
            else:
                cross[i, j] = cx[i] if i else cy[j]
        head = cross[i, j]
        if head is None:
            value = jnp.ones_like(px) if k == 0 else cz[k]
        else:
            value = head if k == 0 else head * cz[k]
        ref[t * 8 : t * 8 + 8, :] = value


def first_kernel(
    me_ref, occ_ref, count_ref, dip_ref, perm_ref, pos_ref, pol_ref, boxes_ref, class_ref, scale_ref, out_ref, mono, chunk
):
    chunk[...] = jnp.zeros_like(chunk)
    lane = lax.broadcasted_iota(jnp.int32, (1, TILE), 1)
    for w in range(2):
        live = (lane < occ_ref[w]).astype(F32)
        lanes = slice(w * TILE, (w + 1) * TILE)
        base = 8 + w * 8
        chunk[base : base + 3, :] = pos_ref[:, lanes]
        chunk[base + 3 : base + 4, :] = pol_ref[:, lanes]
        chunk[base + 4 : base + 7, :] = dip_ref[:, lanes] * live
        chunk[base + 7 : base + 8, :] = live
        chunk[24 + w * 3 : 27 + w * 3, :] = perm_ref[:, lanes]
    plane = lax.rem(me_ref[0], OWNERS) // NX
    box = boxes_ref[...]
    within = box & 1
    layer = (box >> 1) & (OWNERS - 1)
    group = box >> 7
    step = (layer >> 2) - plane
    stack = jnp.where(step == 0, 0, jnp.where(step < 0, 1, 2))
    place = stack * 256 + (((group & 1) * PLANE + (group >> 1) * NX + (layer & 3)) << 3) + within
    place = place.astype(F32)
    kind = class_ref[...].astype(F32)
    entry = lax.broadcasted_iota(jnp.int32, (1, ILIST), 1)
    for w in range(2):
        weight = scale_ref[w : w + 1, :] * (entry < count_ref[w]).astype(F32)
        for n, row in enumerate((place[w : w + 1, :], kind[w : w + 1, :], weight)):
            at = 32 + w * 6 + n * 2
            chunk[at : at + 1, :] = row[:, :TILE]
            chunk[at + 1 : at + 2, 0 : ILIST - TILE] = row[:, TILE:]
    def both(row):
        two = chunk[pl.ds(8 + row, 2, stride=8), :]
        return jnp.concatenate([two, two, two, two], axis=0)

    write_monomials(mono, both(0), both(1), both(2))
    for w in range(2):
        terms = mono[pl.ds(w, NTERM, stride=8), :]
        moment = dot(chunk[12 + w * 8 : 15 + w * 8, :], terms, NT)
        for c in range(3):
            chunk[c * 2 + w : c * 2 + w + 1, :] = moment[c : c + 1, :TILE]
            chunk[6 + w : 7 + w, c * REST : (c + 1) * REST] = moment[c : c + 1, TILE:]
    whole = chunk[...]
    for m in range(PLANE):
        out_ref[m, :, :] = whole


def spread(wide_ref, cols, number, fields):
    for box in range(number):
        for f in fields:
            at = box * 8 + f
            wide_ref[f, box * TILE : (box + 1) * TILE, :] = jnp.broadcast_to(cols[:, at : at + 1], (TILE, TILE))


def write_fields(rows_ref, number, px, py, pz, root, first_layer):
    box = lax.broadcasted_iota(jnp.int32, (number, TILE), 0)
    rows_ref[pl.ds(0, number, stride=8), :] = HALF * (px + 2.0 * (box & 1).astype(F32))
    rows_ref[pl.ds(1, number, stride=8), :] = HALF * py
    rows_ref[pl.ds(2, number, stride=8), :] = HALF * (pz + 2.0 * ((box >> 1) + first_layer).astype(F32))
    rows_ref[pl.ds(3, number, stride=8), :] = root


def root_of(pol):
    return jnp.where(pol > 0.0, ROOT_THOLE * lax.rsqrt(jnp.where(pol > 0.0, pol, 1.0)), 0.0)


def pair(target, source):
    dx, dy, dz = target[0] - source[0], target[1] - source[1], target[2] - source[2]
    squared = dx * dx + dy * dy + (dz * dz + 1.0)
    inverse = lax.rsqrt(squared)
    inv_two = inverse * inverse
    inv_three = inverse * inv_two
    minus = (squared * (squared * inverse)) * (target[3] * source[3])
    damping = jnp.exp(minus)
    lambda_three = 1.0 - damping
    lambda_five = lambda_three + minus * damping
    direct = lambda_three * inv_three
    radial = (3.0 * lambda_five) * (inv_three * inv_two)
    return (dx, dy, dz), radial, direct


def apply_pair(delta, radial, direct, moment, total):
    along = radial * (delta[0] * moment[0] + delta[1] * moment[1] + delta[2] * moment[2])
    return tuple(total[c] + (delta[c] * along - direct * moment[c]) for c in range(3))


def target_rows(rows_ref, box):
    rows = [jnp.broadcast_to(rows_ref[pl.ds(box * 8 + f, 1), :], (8, TILE)) for f in range(4)]
    rows[3] = -rows[3]
    return rows


def near_sum(wide_ref, targets, first_tile, tiles, keep=None, unroll=4):
    zero = tuple(jnp.zeros((8, TILE), F32) for _ in range(6))

    def body(n, total):
        total = [total[:3], total[3:]]
        for u in range(unroll):
            at = pl.ds(pl.multiple_of((first_tile + n * unroll + u) * 8, 8), 8)
            source = [wide_ref[f, at, :] for f in range(4)]
            moment = [wide_ref[f, at, :] for f in range(4, 7)]
            for w in range(2):
                delta, radial, direct = pair(targets[w], source)
                if keep is not None:
                    slot = (n * unroll + u) * 2 + w
                    keep[0, pl.ds(pl.multiple_of(slot * 8, 8), 8), :] = radial
                    keep[1, pl.ds(pl.multiple_of(slot * 8, 8), 8), :] = direct
                total[w] = apply_pair(delta, radial, direct, moment, total[w])
        return tuple(total[0]) + tuple(total[1])

    total = lax.fori_loop(0, tiles // unroll, body, zero)
    return total[:3], total[3:]


def self_term(root):
    return 1.0 - jnp.exp(-(root * root))


def row_sum(x):
    return jnp.sum(x, axis=0, keepdims=True)


def second_kernel(me_ref, block_ref, sel_ref, near_ref, rows, wide):
    mine = (me_ref[0] // (2 * OWNERS)) * NX
    near = [[block_ref[mine + x, 8 + w * 8 : 16 + w * 8, :] for w in range(2)] for x in range(NX)]
    near = jnp.concatenate([near[x][w] for x in range(NX) for w in range(2)], axis=0)
    rows[...] = jnp.zeros_like(rows)
    rows[0:64, :] = near

    def field(f):
        return rows[pl.ds(f, 8, stride=8), :]

    px, py, pz, root = field(0), field(1), field(2), root_of(field(3))
    write_fields(rows, 8, px, py, pz, root, 0)
    spread(wide, jnp.transpose(rows[...]), 8, range(7))
    for layer in range(NX):
        low, high = max(layer - 1, 0), min(layer + 1, NX - 1)
        targets = [target_rows(rows, layer * 2 + w) for w in range(2)]
        totals = near_sum(wide, targets, low * 32, (high - low + 1) * 32)
        for w in range(2):
            for c in range(3):
                near_ref[c * 8 + layer * 2 + w : c * 8 + layer * 2 + w + 1, :] = row_sum(totals[w][c])
    spot = lax.broadcasted_iota(jnp.int32, (768, TILE), 0)
    kinds = lax.broadcasted_iota(jnp.int32, (CLASSES, TILE), 0)
    for x in range(NX):
        for w in range(2):
            total = jnp.zeros((CLASSES, 768), F32)
            for half in range(2):
                at = 32 + w * 6 + half
                place = block_ref[mine + x, at : at + 1, :].astype(jnp.int32)
                kind = block_ref[mine + x, at + 2 : at + 3, :].astype(jnp.int32)
                weight = jnp.where(kinds == kind, block_ref[mine + x, at + 4 : at + 5, :], 0.0)
                chosen = jnp.where(spot == place, 1.0, 0.0).astype(BF16)
                high = weight.astype(BF16)
                left = weight - high.astype(F32)
                middle = left.astype(BF16)
                low = (left - middle.astype(F32)).astype(BF16)
                parts = jnp.concatenate([high.astype(F32), middle.astype(F32), low.astype(F32)], axis=0).astype(BF16)
                got = dot(parts, chosen, NT, None)
                total = total + (got[0:8] + got[8:16] + got[16:24])
            k = x * 2 + w
            sel_ref[k * 8 : k * 8 + 8, :] = total


def third_kernel(
    me_ref, block_ref, own_ref, low_ref, high_ref, sel_ref, near_ref, trans_ref, res_ref, send_ref,
    summed, local, mono, rows, wide, edge,
):
    mine = (me_ref[0] // (2 * OWNERS)) * NX
    x_me = lax.rem(me_ref[0], NX)
    sel = sel_ref[...]
    lhs = jnp.concatenate([sel] + [pltpu.roll(sel, 2 * n, 1) for n in range(1, 4)], axis=0)
    stacked = jnp.concatenate([own_ref[...], low_ref[0:256, :], high_ref[0:256, :]], axis=0)
    summed[...] = dot(lhs, stacked, NN)
    total = jnp.zeros((24, NTERM), F32)
    for o in range(CLASSES):
        rest = summed[pl.ds(192 + o, 8, stride=8), :]
        parts = []
        for c in range(3):
            head = summed[pl.ds(c * 64 + o, 8, stride=8), :]
            parts.append(jnp.concatenate([head, rest[:, c * REST : (c + 1) * REST]], axis=1))
        total = total + dot(jnp.concatenate(parts, axis=0), trans_ref[o], NT)
    local[0:24, :] = total[:, :TILE]
    local[24:48, 0:REST] = total[:, TILE:]
    near = jnp.concatenate([block_ref[mine + x, 8 + w * 8 : 16 + w * 8, :] for x in range(NX) for w in range(2)], axis=0)
    edge_low = low_ref[272:288, :]
    edge_high = high_ref[256:272, :]
    rows[...] = jnp.zeros_like(rows)
    rows[0:16, :] = edge_low
    rows[16:80, :] = near
    rows[80:96, :] = edge_high

    def field(f):
        return rows[pl.ds(f, 12, stride=8), :]

    px, py, pz, pol = field(0), field(1), field(2), field(3)
    live = rows[pl.ds(16 + 7, 8, stride=8), :]
    source = [rows[pl.ds(16 + 4 + c, 8, stride=8), :] for c in range(3)]
    root = root_of(pol)
    write_monomials(mono, px[2:10], py[2:10], pz[2:10])
    write_fields(rows, 12, px, py, pz, root, -1)
    cols = jnp.transpose(rows[...])
    for slot, box in enumerate((0, 1, 10, 11)):
        for f in range(7):
            at = box * 8 + f
            wide[f, slot * TILE : (slot + 1) * TILE, :] = jnp.broadcast_to(cols[:, at : at + 1], (TILE, TILE))
    edge[...] = near_ref[...]
    for side, layer in ((0, 0), (1, NX - 1)):
        targets = [target_rows(rows, 2 + layer * 2 + w) for w in range(2)]
        totals = near_sum(wide, targets, side * 32, 32)
        for w in range(2):
            for c in range(3):
                at = c * 8 + layer * 2 + w
                edge[at : at + 1, :] = edge[at : at + 1, :] + row_sum(totals[w][c])
    far = [[] for _ in range(3)]
    for k in range(8):
        mine_k = jnp.concatenate([local[pl.ds(k, 3, stride=8), :], local[pl.ds(24 + k, 3, stride=8), :][:, 0:REST]], axis=1)
        got = dot(mine_k, mono[pl.ds(k, NTERM, stride=8), :], NN)
        for c in range(3):
            far[c].append(got[c : c + 1, :])
    alone = self_term(root[2:10])
    for c in range(3):
        perm = jnp.concatenate(
            [block_ref[mine + x, 24 + w * 3 + c : 25 + w * 3 + c, :] for x in range(NX) for w in range(2)], axis=0
        )
        near_zero = edge[c * 8 : c * 8 + 8, :] + alone * source[c]
        res_ref[c * 8 : c * 8 + 8, :] = live * (
            perm + jnp.concatenate(far[c], axis=0) + near_zero - source[c] / pol[2:10]
        )
    first = jnp.where(x_me < 2, 4, 0)
    for c in range(3):
        for k in range(4):
            send_ref[c * 4 + k : c * 4 + k + 1, :] = res_ref[pl.ds(c * 8 + first + k, 1), :]


def fourth_kernel(
    me_ref, block_ref, low_ref, high_ref, res_ref, got_ref, new_ref, out_ref, every, rows, moved, wide, keep, field_two
):
    mine = (me_ref[0] // (2 * OWNERS)) * NX
    x_me = lax.rem(me_ref[0], NX)
    every[0:32, :] = low_ref[256:288, :]
    for x in range(NX):
        every[32 + x * 16 : 48 + x * 16, :] = block_ref[mine + x, 8:24, :]
    every[96:128, :] = high_ref[256:288, :]
    for c in range(3):
        got = got_ref[c * 4 : c * 4 + 4, :]
        moved[c, 0:4, :] = got
        moved[c, 4:12, :] = res_ref[c * 8 : c * 8 + 8, :]
        moved[c, 12:16, :] = got
    first = x_me * 2
    rows[...] = jnp.zeros_like(rows)
    for k in range(10):
        rows[k * 8 : k * 8 + 8, :] = every[pl.ds(pl.multiple_of((first + k) * 8, 8), 8), :]

    def field(f):
        return rows[pl.ds(f, 10, stride=8), :]

    px, py, pz, pol, live = field(0), field(1), field(2), field(3), field(7)
    source = [rows[pl.ds(32 + 4 + c, 2, stride=8), :] for c in range(3)]
    residual = [
        jnp.concatenate([moved[c, pl.ds(first + k, 1), :] for k in range(10)], axis=0) for c in range(3)
    ]
    root = root_of(pol)
    alone = self_term(root)
    write_fields(rows, 10, px, py, pz, root, -2)
    one = [pol * residual[c] for c in range(3)]
    for c in range(3):
        rows[pl.ds(4 + c, 10, stride=8), :] = one[c]
    spread(wide, jnp.transpose(rows[...]), 10, range(7))
    for layer in (1, 2, 3):
        targets = [target_rows(rows, layer * 2 + w) for w in range(2)]
        totals = near_sum(wide, targets, (layer - 1) * 32, 96, keep if layer == 2 else None)
        for w in range(2):
            for c in range(3):
                at = (layer - 1) * 2 + w
                field_two[c, at : at + 1, :] = row_sum(totals[w][c])
    two = []
    for c in range(3):
        total = field_two[c, 0:6, :] + alone[2:8] * one[c][2:8]
        two.append(live[2:8] * pol[2:8] * (residual[c][2:8] + total))
        rows[pl.ds(16 + 4 + c, 6, stride=8), :] = two[c]
    cols = jnp.transpose(rows[...])
    for box in range(2, 8):
        for f in range(4, 7):
            at = box * 8 + f
            wide[f, box * TILE : (box + 1) * TILE, :] = jnp.broadcast_to(cols[:, at : at + 1], (TILE, TILE))
    targets = [target_rows(rows, 4 + w) for w in range(2)]

    def body(n, total):
        total = [total[:3], total[3:]]
        for u in range(4):
            tile = n * 4 + u
            at = pl.ds(pl.multiple_of((32 + tile) * 8, 8), 8)
            source_at = [wide[f, at, :] for f in range(3)]
            moment = [wide[f, at, :] for f in range(4, 7)]
            for w in range(2):
                slot = pl.ds(pl.multiple_of((tile * 2 + w) * 8, 8), 8)
                delta = [targets[w][c] - source_at[c] for c in range(3)]
                total[w] = apply_pair(delta, keep[0, slot, :], keep[1, slot, :], moment, total[w])
        return tuple(total[0]) + tuple(total[1])

    final = lax.fori_loop(0, 24, body, tuple(jnp.zeros((8, TILE), F32) for _ in range(6)))
    for c in range(3):
        for w in range(2):
            box = 4 + w
            own = residual[c][box : box + 1]
            total = row_sum(final[w * 3 + c]) + alone[box : box + 1] * two[c][2 + w : 3 + w]
            three = live[box : box + 1] * pol[box : box + 1] * (own + total)
            new_ref[c : c + 1, w * TILE : (w + 1) * TILE] = source[c][w : w + 1] + three
            out_ref[c : c + 1, w * TILE : (w + 1) * TILE] = own


VMEM = pl.BlockSpec(memory_space=pltpu.VMEM)
SMEM = pl.BlockSpec(memory_space=pltpu.SMEM)


def call(body, ins, outs, scratch, cost, name):
    return pl.pallas_call(
        body,
        in_specs=ins,
        out_specs=[VMEM] * len(outs),
        out_shape=[jax.ShapeDtypeStruct(shape, F32) for shape in outs],
        scratch_shapes=[pltpu.VMEM(shape, F32) for shape in scratch],
        cost_estimate=pl.CostEstimate(flops=cost, bytes_accessed=1 << 20, transcendentals=0),
        name=name,
    )


def device(group, box):
    return group * OWNERS + box


def rounds():
    plane = [
        [device(2 * y + core, z * NX + x) for y in range(NY) for x in range(NX)]
        for core in range(2)
        for z in range(OWNERS // NX)
    ]
    chip = [[device(2 * y, b), device(2 * y + 1, b)] for y in range(NY) for b in range(OWNERS)]
    up = [(device(g, b), device(g, b + NX)) for g in range(GROUPS) for b in range(OWNERS - NX)]
    down = [(target, source) for source, target in up]
    near_side = [(s, t) for s, t in up if s % NX < 2] + [(s, t) for s, t in down if s % NX >= 2]
    return plane, chip, up, down, near_side


PLANE_SETS, CHIP_SETS, UP, DOWN, NEAR_SIDE = rounds()


def on_device(
    dipoles, perm_field, positions, polarizability, occupancy, far_boxes, far_class, far_count, far_scale, translations
):
    me = lax.axis_index("d").astype(jnp.int32)[None]
    [chunk] = call(
        first_kernel, [SMEM] * 3 + [VMEM] * 7, [(PLANE, CHUNK, TILE)], [(NTERM * 8, TILE), (CHUNK, TILE)], 1 << 20, "first"
    )(
        me, occupancy, far_count, dipoles, perm_field, positions, polarizability.reshape(1, 2 * TILE),
        far_boxes, far_class, far_scale,
    )
    block = lax.all_to_all(chunk, "d", 0, 0, axis_index_groups=PLANE_SETS, tiled=True)
    own = lax.all_gather(block[:, 0:8, :], "d", axis_index_groups=CHIP_SETS, axis=0).reshape(256, TILE)
    mine = (me[0] // (2 * OWNERS)) * NX
    near = lax.dynamic_slice(block, (mine, 8, 0), (NX, 16, TILE))
    low = lax.ppermute(jnp.concatenate([own, near[2:4].reshape(32, TILE)], axis=0), "d", UP)
    high = lax.ppermute(jnp.concatenate([own, near[0:2].reshape(32, TILE)], axis=0), "d", DOWN)
    sel, near_zero = call(
        second_kernel, [SMEM, VMEM], [(64, 768), (24, TILE)], [(TILE, TILE), (7, 8 * TILE, TILE)], 1 << 26, "second"
    )(me, block)
    residual, send = call(
        third_kernel,
        [SMEM] + [VMEM] * 7,
        [(24, TILE), (12, TILE)],
        [(256, TILE), (48, TILE), (NTERM * 8, TILE), (TILE, TILE), (7, 4 * TILE, TILE), (24, TILE)],
        1 << 26,
        "third",
    )(me, block, own, low, high, sel, near_zero, translations)
    got = lax.ppermute(send, "d", NEAR_SIDE)
    new, out = call(
        fourth_kernel,
        [SMEM] + [VMEM] * 5,
        [(3, 2 * TILE), (3, 2 * TILE)],
        [(TILE, TILE), (TILE, TILE), (3, 16, TILE), (7, 10 * TILE, TILE), (2, 192 * 8, TILE), (3, 8, TILE)],
        1 << 26,
        "fourth",
    )(me, block, low, high, residual, got)
    return new, out


def solution(mesh):
    flat = Mesh(mesh.devices.reshape(-1), ("d",))
    return jax.shard_map(
        on_device,
        mesh=flat,
        in_specs=(
            P(None, "d"), P(None, "d"), P(None, "d"), P("d"), P("d"), P("d", None), P("d", None), P("d"), P("d", None), P(),
        ),
        out_specs=(P(None, "d"), P(None, "d")),
        check_vma=False,
    )
```

time: 119 us -> 63.4 us (0.53)
  the two profiles are of different devices: /device:TPU:102 before, /device:TPU:384 now
where the time goes in v1:
time: 63.4 us; the launch traced here: 63.1 us
  Pallas kernels  27.5 us (43%)
  starting transfers between devices  15.8 us (25%)
  waiting for transfers between devices  14.3 us (23%)
  local copies, waits for them, and re-layouts  2.85 us (4%)
  blocking collectives  1.9 us (3%)
  between operations  0.73 us (1%)
    all_to_all x1, waiting for transfers between devices, on_device(): lax.all_to_all(chunk, 'd', 0, 0, axis_index_groups=PLANE_SETS, tiled=True)  10.1 us
    pallas_call x1, Pallas kernels, on_device(): call(fourth_kernel, [SMEM] + [VMEM] * 5, [(3, 2 * TILE), (3, 2 * TILE)],...  8.71 us
    pallas_call x1, Pallas kernels, on_device(): call(second_kernel, [SMEM, VMEM], [(64, 768), (24, TILE)], [(TILE, TILE),...  8.62 us
    pallas_call x1, Pallas kernels, on_device(): call(third_kernel, [SMEM] + [VMEM] * 7, [(24, TILE), (12, TILE)], [(256,...  7.96 us
    all_to_all x1, starting transfers between devices, on_device(): lax.all_to_all(chunk, 'd', 0, 0, axis_index_groups=PLANE_SETS, tiled=True)  7.03 us
    ppermute x1, waiting for transfers between devices, on_device(): got = lax.ppermute(send, 'd', NEAR_SIDE)  4.23 us
    ppermute x1, starting transfers between devices, on_device(): lax.ppermute(jnp.concatenate([own, near[0:2].reshape(32, TILE)], axis=0),...  4.13 us
    unnamed x13, local copies, waits for them, and re-layouts  2.85 us
  transfers between devices with their start and end apart: 4, of which 2 were waited for; matrix products, arithmetic and copies ran while one was open for 2% of the time, Pallas kernels for 14%

profile of v1, /device:TPU:384, one launch (start us, length us, event | category | flops | bytes accessed | tf_op | source)
XLA Modules:
  0.0 63.1 jit_solution(2695286146343914447)
XLA Ops:
  0.6 0.0 copy-start.1
  0.6 2.2 %first.1 = f32[16,48,128]{2,1,0:T(8,128)} custom-call(s32[1]{0:T(128)} %bitcast.me_ref, s32[2]{0:T(128)} %occ_ref.1, s32[2]{0:T(128)} %count_ref.1, f32[3,256]{1,0:T(4,128)} %dip_ref.1, f32[3,256]{1,0:T(4,128)} %perm_ref.1, f32[3,256]{1,0:T(4,128)} %pos_ref.1, f32[1,256]{1,0:T(1,128)} %bitcast.9, s32[2,189]{1,0:T(2,128)} %boxes_ref.1, s32[2,189]{1,0:T(2,128)} %class_ref.1, ...), custom_call_target="tpu_custom_call" | custom-call | flops 1048576 | bytes 1048576 | tf_op jit(solution)/shard_map/first/pallas_call | solution.py:426
  2.8 7.0 %all-to-all-start = ((f32[16,48,128]{2,1,0:T(8,128)}), f32[16,48,128]{2,1,0:T(8,128)S(1)}, u32[]{:S(2)}, u32[]{:S(2)}) async-start(f32[16,48,128]{2,1,0:T(8,128)} %first.1), calls=%async_computation | async-start | bytes 786432 | tf_op jit(solution)/shard_map/all_to_all | solution.py:432
  9.9 10.1 %all-to-all-done.block_ref = f32[16,48,128]{2,1,0:T(8,128)S(1)} async-done(((f32[16,48,128]{2,1,0:T(8,128)}), f32[16,48,128]{2,1,0:T(8,128)S(1)}, u32[]{:S(2)}, u32[]{:S(2)}) %all-to-all-start) | async-done | bytes 393248 | tf_op jit(solution)/shard_map/all_to_all | solution.py:432
  19.9 0.0 copy-start
  20.0 1.9 %all-gather = f32[32,8,128]{2,1,0:T(8,128)S(1)} all-gather(f32[16,8,128]{2,1,0:T(8,128)S(1)} %slice.12), channel_id=2, replica_groups={{0,64},{1,65},{2,66},{3,67},{4,68},{5,69},{6,70},{7,71},{8,72},{9,73},{..., dimensions={0}, use_global_device_ids=true | all-gather | bytes 196608 | tf_op jit(solution)/shard_map/all_gather | solution.py:433
  21.9 0.0 copy-start.2
  21.9 4.1 %collective-permute-start.1 = (f32[288,128]{1,0:T(8,128)S(1)}, f32[288,128]{1,0:T(8,128)S(1)}, u32[]{:S(2)}, u32[]{:S(2)}) collective-permute-start(f32[288,128]{1,0:T(8,128)S(1)} %get-tuple-element.12), channel_id=1, source_target_pairs={{4,0},{5,1},{6,2},{7,3},{8,4},{9,5},{10,6},{11,7},{12,8},{13,9},{1... | collective-permute-start | bytes 442376 | tf_op jit(solution)/shard_map/ppermute | solution.py:437
  26.0 1.9 %collective-permute-start = (f32[288,128]{1,0:T(8,128)S(1)}, f32[288,128]{1,0:T(8,128)S(1)}, u32[]{:S(2)}, u32[]{:S(2)}) collective-permute-start(f32[288,128]{1,0:T(8,128)S(1)} %get-tuple-element.13), channel_id=1, source_target_pairs={{0,4},{1,5},{2,6},{3,7},{4,8},{5,9},{6,10},{7,11},{8,12},{9,13},{1... | collective-permute-start | bytes 442376 | tf_op jit(solution)/shard_map/ppermute | solution.py:436
  27.9 0.0 copy-done.1
  28.0 1.5 %copy.13.trans_ref = f32[8,165,165]{2,1,0:T(8,128)} copy(f32[8,165,165]{2,0,1:T(8,128)S(1)} %copy-done.1) | data formatting | bytes 1742400 | tf_op args[9]
  29.5 0.0 copy-done
  29.5 0.0 copy-done.2
  29.5 8.6 %second.1 = (f32[64,768]{1,0:T(8,128)}, f32[24,128]{1,0:T(8,128)}) custom-call(s32[1]{0:T(128)} %bitcast.me_ref, f32[16,48,128]{2,1,0:T(8,128)} %copy-done), custom_call_target="tpu_custom_call" | custom-call | flops 67108864 | bytes 1048576 | tf_op jit(solution)/shard_map/second/pallas_call | solution.py:438
  38.1 0.0 collective-permute-done.1.high_ref
  38.1 0.0 copy-start.3
  38.1 0.0 collective-permute-done.low_ref
  38.1 0.0 copy-start.4
  38.1 0.6 %copy-done.3 = f32[288,128]{1,0:T(8,128)} copy-done((f32[288,128]{1,0:T(8,128)}, f32[288,128]{1,0:T(8,128)S(1)}, u32[]{:S(2)}) %copy-start.3) | copy-done | bytes 147480
  38.8 0.1 copy-done.4
  38.8 8.0 %third.1 = (f32[24,128]{1,0:T(8,128)}, f32[12,128]{1,0:T(8,128)}) custom-call(s32[1]{0:T(128)} %bitcast.me_ref, f32[16,48,128]{2,1,0:T(8,128)} %copy-done, f32[256,128]{1,0:T(8,128)} %bitcast.6, f32[288,128]{1,0:T(8,128)} %copy-done.4, f32[288,128]{1,0:T(8,128)} %copy-done.3, f32[64,768]{1,0:T(8,128)} %get-tuple-element.6.sel_ref, ...), custom_call_target="tpu_custom_call" | custom-call | flops 67108864 | bytes 1048576 | tf_op jit(solution)/shard_map/third/pallas_call | solution.py:441
  46.8 2.7 %collective-permute-start.2 = (f32[12,128]{1,0:T(8,128)}, f32[12,128]{1,0:T(8,128)S(1)}, u32[]{:S(2)}, u32[]{:S(2)}) collective-permute-start(f32[12,128]{1,0:T(8,128)} %get-tuple-element.9), channel_id=1, source_target_pairs={{0,4},{1,5},{4,8},{5,9},{8,12},{9,13},{12,16},{13,17},{16,20},{17,... | collective-permute-start | bytes 18440 | tf_op jit(solution)/shard_map/ppermute | solution.py:449
  49.5 4.2 %collective-permute-done.2.got_ref = f32[12,128]{1,0:T(8,128)S(1)} collective-permute-done((f32[12,128]{1,0:T(8,128)}, f32[12,128]{1,0:T(8,128)S(1)}, u32[]{:S(2)}, u32[]{:S(2)}) %collective-permute-start.2) | collective-permute-done | bytes 6176 | tf_op jit(solution)/shard_map/ppermute | solution.py:449
  53.8 0.0 copy-start.5
  53.8 0.6 copy-done.5
  54.4 8.7 %fourth.1 = (f32[3,256]{1,0:T(4,128)}, f32[3,256]{1,0:T(4,128)}) custom-call(s32[1]{0:T(128)} %bitcast.me_ref, f32[16,48,128]{2,1,0:T(8,128)} %copy-done, f32[288,128]{1,0:T(8,128)} %copy-done.4, f32[288,128]{1,0:T(8,128)} %copy-done.3, f32[24,128]{1,0:T(8,128)} %get-tuple-element.8.res_ref, f32[12,128]{1,0:T(8,128)} %copy-done.5), custom_call_target="tpu_custom_call" | custom-call | flops 67108864 | bytes 1048576 | tf_op jit(solution)/shard_map/fourth/pallas_call | solution.py:450
  (3 shorter events, 0.0 us)
Async XLA Ops:
  0.6 27.3 %copy-start.1 = (f32[8,165,165]{2,0,1:T(8,128)S(1)}, f32[8,165,165]{2,0,1:T(8,128)}, u32[]{:S(2)}) copy-start(f32[8,165,165]{2,0,1:T(8,128)} %param.19) | copy-start | bytes 2613604
  2.8 17.1 %all-to-all-start = ((f32[16,48,128]{2,1,0:T(8,128)}), f32[16,48,128]{2,1,0:T(8,128)S(1)}, u32[]{:S(2)}, u32[]{:S(2)}) async-start(f32[16,48,128]{2,1,0:T(8,128)} %first.1), calls=%async_computation | async-start | bytes 786432 | tf_op jit(solution)/shard_map/all_to_all | solution.py:432
  19.9 9.6 %copy-start = (f32[16,48,128]{2,1,0:T(8,128)}, f32[16,48,128]{2,1,0:T(8,128)S(1)}, u32[]{:S(2)}) copy-start(f32[16,48,128]{2,1,0:T(8,128)S(1)} %all-to-all-done.block_ref) | copy-start | bytes 1179652
  21.9 7.6 %copy-start.2 = (f32[32,8,128]{2,1,0:T(8,128)}, f32[32,8,128]{2,1,0:T(8,128)S(1)}, u32[]{:S(2)}) copy-start(f32[32,8,128]{2,1,0:T(8,128)S(1)} %all-gather) | copy-start | bytes 393220
  21.9 16.2 %collective-permute-start.1 = (f32[288,128]{1,0:T(8,128)S(1)}, f32[288,128]{1,0:T(8,128)S(1)}, u32[]{:S(2)}, u32[]{:S(2)}) collective-permute-start(f32[288,128]{1,0:T(8,128)S(1)} %get-tuple-element.12), channel_id=1, source_target_pairs={{4,0},{5,1},{6,2},{7,3},{8,4},{9,5},{10,6},{11,7},{12,8},{13,9},{1... | collective-permute-start | bytes 442376 | tf_op jit(solution)/shard_map/ppermute | solution.py:437
  26.0 12.1 %collective-permute-start = (f32[288,128]{1,0:T(8,128)S(1)}, f32[288,128]{1,0:T(8,128)S(1)}, u32[]{:S(2)}, u32[]{:S(2)}) collective-permute-start(f32[288,128]{1,0:T(8,128)S(1)} %get-tuple-element.13), channel_id=1, source_target_pairs={{0,4},{1,5},{2,6},{3,7},{4,8},{5,9},{6,10},{7,11},{8,12},{9,13},{1... | collective-permute-start | bytes 442376 | tf_op jit(solution)/shard_map/ppermute | solution.py:436
  38.1 0.7 %copy-start.3 = (f32[288,128]{1,0:T(8,128)}, f32[288,128]{1,0:T(8,128)S(1)}, u32[]{:S(2)}) copy-start(f32[288,128]{1,0:T(8,128)S(1)} %collective-permute-done.1.high_ref) | copy-start | bytes 442372
  38.1 0.7 %copy-start.4 = (f32[288,128]{1,0:T(8,128)}, f32[288,128]{1,0:T(8,128)S(1)}, u32[]{:S(2)}) copy-start(f32[288,128]{1,0:T(8,128)S(1)} %collective-permute-done.low_ref) | copy-start | bytes 442372
  46.8 7.0 %collective-permute-start.2 = (f32[12,128]{1,0:T(8,128)}, f32[12,128]{1,0:T(8,128)S(1)}, u32[]{:S(2)}, u32[]{:S(2)}) collective-permute-start(f32[12,128]{1,0:T(8,128)} %get-tuple-element.9), channel_id=1, source_target_pairs={{0,4},{1,5},{4,8},{5,9},{8,12},{9,13},{12,16},{13,17},{16,20},{17,... | collective-permute-start | bytes 18440 | tf_op jit(solution)/shard_map/ppermute | solution.py:449
  53.8 0.6 copy-start.5

commit v2 on v1

v2 whole, which is shorter than its diff:
```python
import jax
import jax.numpy as jnp
from jax import lax
from jax.experimental import pallas as pl
from jax.experimental.pallas import tpu as pltpu
from jax.sharding import Mesh
from jax.sharding import PartitionSpec as P

TILE = 128
ORDER = 8
NTERM = 165
REST = NTERM - TILE
ILIST = 189
CLASSES = 8
GROUPS = 8
OWNERS = 64
NX = 4
NY = 4
PLANE = NX * NY
CHUNK = 48
F32 = jnp.float32
BF16 = jnp.bfloat16

HALF = 5.4
ROOT_THOLE = 0.39**0.5
NT = (((1,), (1,)), ((), ()))
NN = (((1,), (0,)), ((), ()))


def term_table():
    listing = []
    for degree in range(ORDER + 1):
        for first in range(degree + 1):
            for second in range(degree + 1 - first):
                listing.append((first, second, degree - first - second))
    return listing


TERMS = term_table()


def dot(a, b, dims):
    return lax.dot_general(a, b, dims, preferred_element_type=F32)


def halves(x):
    high = x.astype(BF16)
    return high, (x - high.astype(F32)).astype(BF16)


def dot_three(a, b, dims):
    a_high, a_low = halves(a)
    b_high, b_low = halves(b)
    return dot(a_high, b_high, dims) + (dot(a_high, b_low, dims) + dot(a_low, b_high, dims))


def chebyshev(coord):
    series = [None, coord]
    doubled = 2.0 * coord
    series.append(doubled * coord - 1.0)
    for _ in range(3, ORDER + 1):
        series.append(doubled * series[-1] - series[-2])
    return series


def write_monomials(ref, px, py, pz):
    cx, cy, cz = chebyshev(px), chebyshev(py), chebyshev(pz)
    cross = {}
    for t, (i, j, k) in enumerate(TERMS):
        if (i, j) not in cross:
            if i and j:
                cross[i, j] = cx[i] * cy[j]
            else:
                cross[i, j] = cx[i] if i else cy[j]
        head = cross[i, j]
        if head is None:
            value = jnp.ones_like(px) if k == 0 else cz[k]
        else:
            value = head if k == 0 else head * cz[k]
        ref[t * 8 : t * 8 + 8, :] = value


def first_kernel(
    me_ref, occ_ref, count_ref, dip_ref, perm_ref, pos_ref, pol_ref, boxes_ref, class_ref, scale_ref, out_ref, mono, chunk
):
    chunk[...] = jnp.zeros_like(chunk)
    lane = lax.broadcasted_iota(jnp.int32, (1, TILE), 1)
    for w in range(2):
        live = (lane < occ_ref[w]).astype(F32)
        lanes = slice(w * TILE, (w + 1) * TILE)
        base = 8 + w * 8
        chunk[base : base + 3, :] = pos_ref[:, lanes]
        chunk[base + 3 : base + 4, :] = pol_ref[:, lanes]
        chunk[base + 4 : base + 7, :] = dip_ref[:, lanes] * live
        chunk[base + 7 : base + 8, :] = live
        chunk[24 + w * 3 : 27 + w * 3, :] = perm_ref[:, lanes]
    plane = lax.rem(me_ref[0], OWNERS) // NX
    box = boxes_ref[...]
    within = box & 1
    layer = (box >> 1) & (OWNERS - 1)
    group = box >> 7
    step = (layer >> 2) - plane
    stack = jnp.where(step == 0, 0, jnp.where(step < 0, 1, 2))
    place = within * 96 + stack * 32 + (group & 1) * PLANE + (group >> 1) * NX + (layer & 3)
    place = place.astype(F32)
    kind = class_ref[...].astype(F32)
    entry = lax.broadcasted_iota(jnp.int32, (1, ILIST), 1)
    for w in range(2):
        weight = scale_ref[w : w + 1, :] * (entry < count_ref[w]).astype(F32)
        for n, row in enumerate((place[w : w + 1, :], kind[w : w + 1, :], weight)):
            at = 32 + w * 6 + n * 2
            chunk[at : at + 1, :] = row[:, :TILE]
            chunk[at + 1 : at + 2, 0 : ILIST - TILE] = row[:, TILE:]
    def both(row):
        two = chunk[pl.ds(8 + row, 2, stride=8), :]
        return jnp.concatenate([two, two, two, two], axis=0)

    write_monomials(mono, both(0), both(1), both(2))
    for w in range(2):
        terms = mono[pl.ds(w, NTERM, stride=8), :]
        moment = dot_three(chunk[12 + w * 8 : 15 + w * 8, :], terms, NT)
        for c in range(3):
            chunk[c * 2 + w : c * 2 + w + 1, :] = moment[c : c + 1, :TILE]
            chunk[6 + w : 7 + w, c * REST : (c + 1) * REST] = moment[c : c + 1, TILE:]
    whole = chunk[...]
    for m in range(PLANE):
        out_ref[m, :, :] = whole


def spread(wide_ref, cols, boxes, fields):
    for slot, box in enumerate(boxes):
        for f in fields:
            at = box * 8 + f
            wide_ref[f, slot * TILE : (slot + 1) * TILE, :] = jnp.broadcast_to(cols[:, at : at + 1], (TILE, TILE))


def write_fields(rows_ref, number, px, py, pz, root, first_layer):
    box = lax.broadcasted_iota(jnp.int32, (number, TILE), 0)
    rows_ref[pl.ds(0, number, stride=8), :] = HALF * (px + 2.0 * (box & 1).astype(F32))
    rows_ref[pl.ds(1, number, stride=8), :] = HALF * py
    rows_ref[pl.ds(2, number, stride=8), :] = HALF * (pz + 2.0 * ((box >> 1) + first_layer).astype(F32))
    rows_ref[pl.ds(3, number, stride=8), :] = root


def root_of(pol):
    return jnp.where(pol > 0.0, ROOT_THOLE * lax.rsqrt(jnp.where(pol > 0.0, pol, 1.0)), 0.0)


def scalars(delta, roots):
    dx, dy, dz = delta
    squared = dx * dx + dy * dy + (dz * dz + 1.0)
    inverse = lax.rsqrt(squared)
    inv_two = inverse * inverse
    inv_three = inverse * inv_two
    minus = -((squared * (squared * inverse)) * roots)
    damping = jnp.exp(minus)
    lambda_three = 1.0 - damping
    lambda_five = lambda_three + minus * damping
    return (3.0 * lambda_five) * (inv_three * inv_two), lambda_three * inv_three


def field_of(delta, radial, direct, moment):
    along = radial * (delta[0] * moment[0] + delta[1] * moment[1] + delta[2] * moment[2])
    return [delta[c] * along - direct * moment[c] for c in range(3)]


def added(parts):
    while len(parts) > 1:
        parts = [parts[i] + parts[i + 1] if i + 1 < len(parts) else parts[i] for i in range(0, len(parts), 2)]
    return parts[0]


def row(ref, at):
    return ref[pl.ds(at, 8, stride=0), :]


def tile_at(n, base=0):
    return pl.ds(pl.multiple_of(base + n * 8, 8), 8)


def trips_of(live):
    count = jnp.sum(live, axis=1, keepdims=True)
    return ((count + 7.0) * 0.125).astype(jnp.int32)


def near_box(total_ref, slot, wide_ref, target, trips, rows_ref, sources):
    def body(n, carry):
        at = tile_at(n, target * TILE)
        mine = [wide_ref[f, at, :] for f in range(4)]
        parts = []
        for box in sources:
            delta = [mine[c] - row(rows_ref, box * 8 + c) for c in range(3)]
            radial, direct = scalars(delta, mine[3] * row(rows_ref, box * 8 + 3))
            parts.append(field_of(delta, radial, direct, [row(rows_ref, box * 8 + 4 + c) for c in range(3)]))
        for c in range(3):
            total_ref[c, tile_at(n, slot * TILE), :] = added([part[c] for part in parts])
        return carry

    lax.fori_loop(0, trips, body, 0)


def lane_sums(total_ref, c, slot):
    return jnp.sum(jnp.transpose(total_ref[c, slot * TILE : (slot + 1) * TILE, :]), axis=0, keepdims=True)


def self_term(root):
    return 1.0 - jnp.exp(-(root * root))


def prepare_kernel(trans_ref, high_ref, low_ref):
    high_ref[...] = jnp.zeros_like(high_ref)
    low_ref[...] = jnp.zeros_like(low_ref)
    for o in range(CLASSES):
        high, low = halves(jnp.transpose(trans_ref[:, o, :]))
        high_ref[o * 256 : o * 256 + NTERM, :] = high
        low_ref[o * 256 : o * 256 + NTERM, :] = low


def second_kernel(me_ref, block_ref, sel_ref, near_ref, wide, rows, total):
    mine = (me_ref[0] // (2 * OWNERS)) * NX
    rows[...] = jnp.zeros_like(rows)
    for x in range(NX):
        rows[x * 16 : x * 16 + 16, :] = block_ref[mine + x, 8:24, :]

    def field(f):
        return rows[pl.ds(f, 8, stride=8), :]

    px, py, pz, root = field(0), field(1), field(2), root_of(field(3))
    trips = trips_of(field(7))
    write_fields(rows, 8, px, py, pz, root, 0)
    spread(wide, jnp.transpose(rows[...]), range(8), range(4))
    for box in range(8):
        low, high = max(box // 2 - 1, 0), min(box // 2 + 1, NX - 1)
        near_box(total, box, wide, box, trips[box, 0], rows, range(low * 2, high * 2 + 2))
    spot = lax.broadcasted_iota(jnp.int32, (192, TILE), 0)
    kinds = lax.broadcasted_iota(jnp.int32, (CLASSES, TILE), 0)
    for k in range(8):
        got = jnp.zeros((16, 192), F32)
        for half in range(2):
            at = 32 + (k % 2) * 6 + half
            place = block_ref[mine + k // 2, at : at + 1, :].astype(jnp.int32)
            kind = block_ref[mine + k // 2, at + 2 : at + 3, :].astype(jnp.int32)
            weight = jnp.where(kinds == kind, block_ref[mine + k // 2, at + 4 : at + 5, :], 0.0)
            chosen = jnp.where(spot == place, 1.0, 0.0).astype(BF16)
            high = weight.astype(BF16).astype(F32)
            parts = jnp.concatenate([high, weight - high], axis=0).astype(BF16)
            got = got + dot(parts, chosen, NT)
        sel_ref[k * 8 : k * 8 + 8, :] = got[0:8] + got[8:16]
    for c in range(3):
        for box in range(8):
            near_ref[c * 8 + box : c * 8 + box + 1, :] = lane_sums(total, c, box)


def third_kernel(
    me_ref, block_ref, own_ref, low_ref, high_ref, sel_ref, near_ref, wide_ref, t_high_ref, t_low_ref, res_ref, send_ref,
    summed, local, mono, rows, total,
):
    mine = (me_ref[0] // (2 * OWNERS)) * NX
    x_me = lax.rem(me_ref[0], NX)
    sel_high, sel_low = halves(sel_ref[...])
    both = jnp.concatenate([sel_high, sel_low], axis=0)
    for kind in range(4):
        flat = jnp.concatenate(
            [ref[pl.ds(kind * 2 + w, 32, stride=8), :] for w in range(2) for ref in (own_ref, low_ref, high_ref)], axis=0
        )
        high, low = halves(flat)
        got = dot(both, high, NN)
        summed[kind * 64 : kind * 64 + 64, :] = got[0:64] + (got[64:128] + dot(sel_high, low, NN))
    parts = []
    for c in range(3):
        pieces = []
        for o in range(CLASSES):
            pieces.append(summed[pl.ds(c * 64 + o, 8, stride=8), :])
            rest = summed[pl.ds(192 + o, 8, stride=8), :][:, c * REST : (c + 1) * REST]
            pieces.append(jnp.concatenate([rest, jnp.zeros((8, TILE - REST), F32)], axis=1))
        parts.append(jnp.concatenate(pieces, axis=1))
    high, low = halves(jnp.concatenate(parts, axis=0))
    t_high, t_low = t_high_ref[...], t_low_ref[...]
    moved = dot(high, t_high, NN) + (dot(low, t_high, NN) + dot(high, t_low, NN))
    local[:, 0:NTERM] = moved
    rows[...] = jnp.zeros_like(rows)
    rows[0:16, :] = low_ref[272:288, :]
    for x in range(NX):
        rows[16 + x * 16 : 32 + x * 16, :] = block_ref[mine + x, 8:24, :]
    rows[80:96, :] = high_ref[256:272, :]

    def field(f):
        return rows[pl.ds(f, 12, stride=8), :]

    px, py, pz, pol = field(0), field(1), field(2), field(3)
    live = rows[pl.ds(16 + 7, 8, stride=8), :]
    source = [rows[pl.ds(16 + 4 + c, 8, stride=8), :] for c in range(3)]
    root = root_of(pol)
    trips = trips_of(live)
    write_monomials(mono, px[2:10], py[2:10], pz[2:10])
    write_fields(rows, 12, px, py, pz, root, -1)
    for slot, box, sources in ((0, 0, (0, 1)), (1, 1, (0, 1)), (2, 6, (10, 11)), (3, 7, (10, 11))):
        near_box(total, slot, wide_ref, box, trips[box, 0], rows, sources)
    far = [jnp.zeros((8, TILE), F32) for _ in range(3)]
    for t in range(NTERM):
        term = mono[t * 8 : t * 8 + 8, :]
        for c in range(3):
            far[c] = far[c] + jnp.broadcast_to(local[c * 8 : c * 8 + 8, t : t + 1], (8, TILE)) * term
    alone = self_term(root[2:10])
    nothing = jnp.zeros((4, TILE), F32)
    for c in range(3):
        perm = jnp.concatenate(
            [block_ref[mine + x, 24 + w * 3 + c : 25 + w * 3 + c, :] for x in range(NX) for w in range(2)], axis=0
        )
        ends = [lane_sums(total, c, slot) for slot in range(4)]
        edge = jnp.concatenate(ends[0:2] + [nothing] + ends[2:4], axis=0)
        near_zero = near_ref[c * 8 : c * 8 + 8, :] + edge + alone * source[c]
        res_ref[c * 8 : c * 8 + 8, :] = jnp.where(
            live > 0.0, perm + far[c] + near_zero - source[c] / pol[2:10], 0.0
        )
    first = jnp.where(x_me < 2, 4, 0)
    for c in range(3):
        for k in range(4):
            send_ref[c * 4 + k : c * 4 + k + 1, :] = res_ref[pl.ds(c * 8 + first + k, 1), :]


def window_kernel(me_ref, block_ref, low_ref, high_ref, rows, keep, wide, every):
    mine = (me_ref[0] // (2 * OWNERS)) * NX
    first = lax.rem(me_ref[0], NX) * 2
    every[0:32, :] = low_ref[256:288, :]
    for x in range(NX):
        every[32 + x * 16 : 48 + x * 16, :] = block_ref[mine + x, 8:24, :]
    every[96:128, :] = high_ref[256:288, :]
    rows[...] = jnp.zeros_like(rows)
    for k in range(10):
        rows[k * 8 : k * 8 + 8, :] = every[pl.ds(pl.multiple_of((first + k) * 8, 8), 8), :]

    def field(f):
        return rows[pl.ds(f, 10, stride=8), :]

    px, py, pz, pol, live = field(0), field(1), field(2), field(3), field(7)
    root = root_of(pol)
    rows[80:90, :] = pol
    rows[96:106, :] = self_term(root)
    trips = trips_of(live)
    write_fields(rows, 10, px, py, pz, root, -2)
    spread(wide, jnp.transpose(rows[...]), range(2, 8), range(4))
    for box in range(2, 8):

        def body(n, carry):
            at = tile_at(n, (box - 2) * TILE)
            spot = [wide[f, at, :] for f in range(4)]
            for k in range(6):
                source = (box // 2 - 1) * 2 + k
                delta = [spot[c] - row(rows, source * 8 + c) for c in range(3)]
                radial, direct = scalars(delta, spot[3] * row(rows, source * 8 + 3))
                keep[k, at, :] = radial
                keep[6 + k, at, :] = direct
            return carry

        lax.fori_loop(0, trips[box, 0], body, 0)


def fourth_kernel(me_ref, rows_ref, keep_ref, wide_ref, res_ref, got_ref, new_ref, out_ref, moved, rows, total):
    first = lax.rem(me_ref[0], NX) * 2
    for c in range(3):
        got = got_ref[c * 4 : c * 4 + 4, :]
        moved[c, 0:4, :] = got
        moved[c, 4:12, :] = res_ref[c * 8 : c * 8 + 8, :]
        moved[c, 12:16, :] = got
    rows[...] = rows_ref[...]
    pol, alone = rows[80:90, :], rows[96:106, :]
    live = rows[pl.ds(7, 10, stride=8), :]
    trips = trips_of(live)
    source = [rows[pl.ds(32 + 4 + c, 2, stride=8), :] for c in range(3)]
    residual = [jnp.concatenate([moved[c, pl.ds(first + k, 1), :] for k in range(10)], axis=0) for c in range(3)]

    def sweep(boxes, moments):
        for c in range(3):
            rows[pl.ds(4 + c, 10, stride=8), :] = moments[c]
        for box in boxes:

            def body(n, carry):
                at = tile_at(n, (box - 2) * TILE)
                spot = [wide_ref[c, at, :] for c in range(3)]
                parts = []
                for k in range(6):
                    near = (box // 2 - 1) * 2 + k
                    delta = [spot[c] - row(rows, near * 8 + c) for c in range(3)]
                    moment = [row(rows, near * 8 + 4 + c) for c in range(3)]
                    parts.append(field_of(delta, keep_ref[k, at, :], keep_ref[6 + k, at, :], moment))
                for c in range(3):
                    total[c, at, :] = added([part[c] for part in parts])
                return carry

            lax.fori_loop(0, trips[box, 0], body, 0)
        return [jnp.concatenate([lane_sums(total, c, box - 2) for box in boxes], axis=0) for c in range(3)]

    one = [pol * residual[c] for c in range(3)]
    fields = sweep(range(2, 8), one)
    two = []
    edge = jnp.zeros((2, TILE), F32)
    for c in range(3):
        value = pol[2:8] * (residual[c][2:8] + fields[c] + alone[2:8] * one[c][2:8])
        two.append(jnp.concatenate([edge, jnp.where(live[2:8] > 0.0, value, 0.0), edge], axis=0))
    fields = sweep(range(4, 6), two)
    for c in range(3):
        value = pol[4:6] * (residual[c][4:6] + fields[c] + alone[4:6] * two[c][4:6])
        three = source[c] + jnp.where(live[4:6] > 0.0, value, 0.0)
        for w in range(2):
            new_ref[c : c + 1, w * TILE : (w + 1) * TILE] = three[w : w + 1]
            out_ref[c : c + 1, w * TILE : (w + 1) * TILE] = residual[c][4 + w : 5 + w]


VMEM = pl.BlockSpec(memory_space=pltpu.VMEM)
SMEM = pl.BlockSpec(memory_space=pltpu.SMEM)


def shape_of(shape):
    return shape if isinstance(shape, jax.ShapeDtypeStruct) else jax.ShapeDtypeStruct(shape, F32)


def call(body, ins, outs, scratch, cost, limit, name):
    return pl.pallas_call(
        body,
        in_specs=ins,
        out_specs=[VMEM] * len(outs),
        out_shape=[shape_of(shape) for shape in outs],
        scratch_shapes=[pltpu.VMEM(shape, F32) for shape in scratch],
        cost_estimate=pl.CostEstimate(flops=cost, bytes_accessed=1 << 20, transcendentals=0),
        compiler_params=pltpu.CompilerParams(vmem_limit_bytes=limit << 20),
        name=name,
    )


def device(group, box):
    return group * OWNERS + box


def rounds():
    plane = [
        [device(2 * y + core, z * NX + x) for y in range(NY) for x in range(NX)]
        for core in range(2)
        for z in range(OWNERS // NX)
    ]
    chip = [[device(2 * y, b), device(2 * y + 1, b)] for y in range(NY) for b in range(OWNERS)]
    up = [(device(g, b), device(g, b + NX)) for g in range(GROUPS) for b in range(OWNERS - NX)]
    down = [(target, source) for source, target in up]
    near_side = [(s, t) for s, t in up if s % NX < 2] + [(s, t) for s, t in down if s % NX >= 2]
    return plane, chip, up, down, near_side


PLANE_SETS, CHIP_SETS, UP, DOWN, NEAR_SIDE = rounds()


def on_device(
    dipoles, perm_field, positions, polarizability, occupancy, far_boxes, far_class, far_count, far_scale, translations
):
    me = lax.axis_index("d").astype(jnp.int32)[None]
    [chunk] = call(
        first_kernel, [SMEM] * 3 + [VMEM] * 7, [(PLANE, CHUNK, TILE)], [(NTERM * 8, TILE), (CHUNK, TILE)], 1 << 20, 8, "first"
    )(
        me, occupancy, far_count, dipoles, perm_field, positions, polarizability.reshape(1, 2 * TILE),
        far_boxes, far_class, far_scale,
    )
    block = lax.all_to_all(chunk, "d", 0, 0, axis_index_groups=PLANE_SETS, tiled=True)
    half = jax.ShapeDtypeStruct((CLASSES * 256, NTERM), BF16)
    t_high, t_low = call(prepare_kernel, [VMEM], [half, half], [], 1 << 28, 12, "prepare")(
        jnp.transpose(translations, (1, 0, 2))
    )
    own = lax.all_gather(block[:, 0:8, :], "d", axis_index_groups=CHIP_SETS, axis=0).reshape(256, TILE)
    mine = (me[0] // (2 * OWNERS)) * NX
    near = lax.dynamic_slice(block, (mine, 8, 0), (NX, 16, TILE))
    low = lax.ppermute(jnp.concatenate([own, near[2:4].reshape(32, TILE)], axis=0), "d", UP)
    high = lax.ppermute(jnp.concatenate([own, near[0:2].reshape(32, TILE)], axis=0), "d", DOWN)
    sel, near_zero, wide = call(
        second_kernel,
        [SMEM, VMEM],
        [(64, 192), (24, TILE), (4, 8 * TILE, TILE)],
        [(TILE, TILE), (3, 8 * TILE, TILE)],
        1 << 28,
        12,
        "second",
    )(me, block)
    residual, send = call(
        third_kernel,
        [SMEM] + [VMEM] * 9,
        [(24, TILE), (12, TILE)],
        [(256, TILE), (24, 256), (NTERM * 8, TILE), (TILE, TILE), (3, 4 * TILE, TILE)],
        1 << 28,
        16,
        "third",
    )(me, block, own, low, high, sel, near_zero, wide, t_high, t_low)
    got = lax.ppermute(send, "d", NEAR_SIDE)
    rows, keep, spread_out = call(
        window_kernel,
        [SMEM] + [VMEM] * 3,
        [(TILE, TILE), (12, 6 * TILE, TILE), (4, 6 * TILE, TILE)],
        [(TILE, TILE)],
        1 << 28,
        16,
        "window",
    )(me, block, low, high)
    new, out = call(
        fourth_kernel,
        [SMEM] + [VMEM] * 5,
        [(3, 2 * TILE), (3, 2 * TILE)],
        [(3, 16, TILE), (TILE, TILE), (3, 6 * TILE, TILE)],
        1 << 28,
        16,
        "fourth",
    )(me, rows, keep, spread_out, residual, got)
    return new, out


def solution(mesh):
    flat = Mesh(mesh.devices.reshape(-1), ("d",))
    return jax.shard_map(
        on_device,
        mesh=flat,
        in_specs=(
            P(None, "d"), P(None, "d"), P(None, "d"), P("d"), P("d"), P("d", None), P("d", None), P("d"), P("d", None), P(),
        ),
        out_specs=(P(None, "d"), P(None, "d")),
        check_vma=False,
    )
```

time: 63.4 us -> 55 us (0.87)
  the two profiles are of different devices: /device:TPU:384 before, /device:TPU:224 now
where the time goes in v2:
time: 55 us; the launch traced here: 54 us
  starting transfers between devices  18.4 us (33%)
  Pallas kernels  16.7 us (30%)
  waiting for transfers between devices  10.1 us (18%)
  local copies, waits for them, and re-layouts  6.2 us (11%)
  blocking collectives  1.89 us (3%)
  between operations  0.76 us (1%)
    all_to_all x1, waiting for transfers between devices, on_device(): lax.all_to_all(chunk, 'd', 0, 0, axis_index_groups=PLANE_SETS, tiled=True)  10.1 us
    all_to_all x1, starting transfers between devices, on_device(): lax.all_to_all(chunk, 'd', 0, 0, axis_index_groups=PLANE_SETS, tiled=True)  7.03 us
    unnamed x20, local copies, waits for them, and re-layouts  6.19 us
    ppermute x1, starting transfers between devices, on_device(): lax.ppermute(jnp.concatenate([own, near[2:4].reshape(32, TILE)], axis=0),...  5.04 us
    pallas_call x1, Pallas kernels, on_device(): call(second_kernel, [SMEM, VMEM], [(64, 192), (24, TILE), (4, 8 * TILE, T...  4.54 us
    ppermute x1, starting transfers between devices, on_device(): got = lax.ppermute(send, 'd', NEAR_SIDE)  4.27 us
    pallas_call x1, Pallas kernels, on_device(): call(third_kernel, [SMEM] + [VMEM] * 9, [(24, TILE), (12, TILE)], [(256,...  3.57 us
    pallas_call x1, Pallas kernels, on_device(): call(fourth_kernel, [SMEM] + [VMEM] * 5, [(3, 2 * TILE), (3, 2 * TILE)],...  3.27 us
  transfers between devices with their start and end apart: 4, of which 1 were waited for; matrix products, arithmetic and copies ran while one was open for 0% of the time, Pallas kernels for 15%

profile of v2, /device:TPU:224, one launch (start us, length us, event | category | flops | bytes accessed | tf_op | source)
XLA Modules:
  0.0 54.0 jit_solution(13436917940676301779)
XLA Ops:
  0.6 0.0 copy-start
  0.6 0.0 copy-start.1
  0.7 0.8 %copy-done.1 = f32[3,256]{1,0:T(4,128)S(1)} copy-done((f32[3,256]{1,0:T(4,128)S(1)}, f32[3,256]{1,0:T(4,128)}, u32[]{:S(2)}) %copy-start.1) | copy-done | bytes 3096
  1.4 0.0 copy-start.2
  1.4 0.7 %copy-done.2 = f32[3,256]{1,0:T(4,128)S(1)} copy-done((f32[3,256]{1,0:T(4,128)S(1)}, f32[3,256]{1,0:T(4,128)}, u32[]{:S(2)}) %copy-start.2) | copy-done | bytes 3096
  2.1 0.0 copy-start.3
  2.1 0.7 %copy-done.3 = f32[3,256]{1,0:T(4,128)S(1)} copy-done((f32[3,256]{1,0:T(4,128)S(1)}, f32[3,256]{1,0:T(4,128)}, u32[]{:S(2)}) %copy-start.3) | copy-done | bytes 3096
  2.8 0.0 copy-start.4
  2.8 0.7 %copy-done.4 = s32[2,189]{1,0:T(2,128)S(1)} copy-done((s32[2,189]{1,0:T(2,128)S(1)}, s32[2,189]{1,0:T(2,128)}, u32[]{:S(2)}) %copy-start.4) | copy-done | bytes 1536
  3.5 0.0 copy-start.5
  3.5 0.7 %copy-done.5 = s32[2,189]{1,0:T(2,128)S(1)} copy-done((s32[2,189]{1,0:T(2,128)S(1)}, s32[2,189]{1,0:T(2,128)}, u32[]{:S(2)}) %copy-start.5) | copy-done | bytes 1536
  4.2 0.0 copy-start.6
  4.2 0.7 %copy-done.6 = f32[2,189]{1,0:T(2,128)S(1)} copy-done((f32[2,189]{1,0:T(2,128)S(1)}, f32[2,189]{1,0:T(2,128)}, u32[]{:S(2)}) %copy-start.6) | copy-done | bytes 1536
  4.9 0.0 copy-start.7
  4.9 0.7 %copy-done.7 = f32[256]{0:T(256)S(1)} copy-done((f32[256]{0:T(256)S(1)}, f32[256]{0:T(256)}, u32[]{:S(2)}) %copy-start.7) | copy-done | bytes 1048
  5.5 0.0 copy-start.8
  5.5 0.7 %copy-done.8 = s32[2]{0:T(128)S(1)} copy-done((s32[2]{0:T(128)S(1)}, s32[2]{0:T(128)}, u32[]{:S(2)}) %copy-start.8) | copy-done | bytes 32
  6.2 0.0 copy-start.9
  6.2 0.7 %copy-done.9 = s32[2]{0:T(128)S(1)} copy-done((s32[2]{0:T(128)S(1)}, s32[2]{0:T(128)}, u32[]{:S(2)}) %copy-start.9) | copy-done | bytes 32
  6.9 1.7 %first.1 = f32[16,48,128]{2,1,0:T(8,128)} custom-call(s32[1]{0:T(128)} %bitcast.me_ref, s32[2]{0:T(128)S(1)} %copy-done.8, s32[2]{0:T(128)S(1)} %copy-done.9, f32[3,256]{1,0:T(4,128)S(1)} %copy-done.1, f32[3,256]{1,0:T(4,128)S(1)} %copy-done.2, f32[3,256]{1,0:T(4,128)S(1)} %copy-done.3, f32[1,256]{1,0:T(1,128)S(1)} %bitcast.9, s32[2,189]{1,0:T(2,128)S(1)} %copy-done.4, ...), custom_call_target="tpu_custom_call" | custom-call | flops 1048576 | bytes 1048576 | tf_op jit(solution)/shard_map/first/pallas_call | solution.py:455
  8.6 7.0 %all-to-all-start = ((f32[16,48,128]{2,1,0:T(8,128)}), f32[16,48,128]{2,1,0:T(8,128)S(1)}, u32[]{:S(2)}, u32[]{:S(2)}) async-start(f32[16,48,128]{2,1,0:T(8,128)} %first.1), calls=%async_computation | async-start | bytes 786432 | tf_op jit(solution)/shard_map/all_to_all | solution.py:461
  15.6 10.1 %all-to-all-done.block_ref = f32[16,48,128]{2,1,0:T(8,128)S(1)} async-done(((f32[16,48,128]{2,1,0:T(8,128)}), f32[16,48,128]{2,1,0:T(8,128)S(1)}, u32[]{:S(2)}, u32[]{:S(2)}) %all-to-all-start) | async-done | bytes 393248 | tf_op jit(solution)/shard_map/all_to_all | solution.py:461
  25.7 1.9 %all-gather = f32[32,8,128]{2,1,0:T(8,128)S(1)} all-gather(f32[16,8,128]{2,1,0:T(8,128)S(1)} %slice.12), channel_id=2, replica_groups={{0,64},{1,65},{2,66},{3,67},{4,68},{5,69},{6,70},{7,71},{8,72},{9,73},{..., dimensions={0}, use_global_device_ids=true | all-gather | bytes 196608 | tf_op jit(solution)/shard_map/all_gather | solution.py:466
  27.6 2.0 %collective-permute-start.1 = (f32[288,128]{1,0:T(8,128)S(1)}, f32[288,128]{1,0:T(8,128)S(1)}, u32[]{:S(2)}, u32[]{:S(2)}) collective-permute-start(f32[288,128]{1,0:T(8,128)S(1)} %get-tuple-element.24), channel_id=1, source_target_pairs={{4,0},{5,1},{6,2},{7,3},{8,4},{9,5},{10,6},{11,7},{12,8},{13,9},{1... | collective-permute-start | bytes 442376 | tf_op jit(solution)/shard_map/ppermute | solution.py:470
  29.6 5.0 %collective-permute-start = (f32[288,128]{1,0:T(8,128)S(1)}, f32[288,128]{1,0:T(8,128)S(1)}, u32[]{:S(2)}, u32[]{:S(2)}) collective-permute-start(f32[288,128]{1,0:T(8,128)S(1)} %get-tuple-element.25), channel_id=1, source_target_pairs={{0,4},{1,5},{2,6},{3,7},{4,8},{5,9},{6,10},{7,11},{8,12},{9,13},{1... | collective-permute-start | bytes 442376 | tf_op jit(solution)/shard_map/ppermute | solution.py:469
  34.7 0.0 copy-done
  34.7 0.8 %prepare.1 = (bf16[2048,165]{1,0:T(8,128)(2,1)S(1)}, bf16[2048,165]{1,0:T(8,128)(2,1)S(1)}) custom-call(f32[165,8,165]{2,1,0:T(8,128)S(1)} %bitcast.6), custom_call_target="tpu_custom_call" | custom-call | flops 268435456 | bytes 1048576 | tf_op jit(solution)/shard_map/prepare/pallas_call | solution.py:463
  35.5 4.5 %second.1 = (f32[64,192]{1,0:T(8,128)S(1)}, f32[24,128]{1,0:T(8,128)S(1)}, f32[4,1024,128]{2,1,0:T(8,128)S(1)}) custom-call(s32[1]{0:T(128)} %bitcast.me_ref, f32[16,48,128]{2,1,0:T(8,128)S(1)} %all-to-all-done.block_ref), custom_call_target="tpu_custom_call" | custom-call | flops 268435456 | bytes 1048576 | tf_op jit(solution)/shard_map/second/pallas_call | solution.py:471
  40.0 0.0 collective-permute-done.1.high_ref
  40.0 0.0 collective-permute-done.low_ref
  40.0 3.6 %third.1 = (f32[24,128]{1,0:T(8,128)S(1)}, f32[12,128]{1,0:T(8,128)S(1)}) custom-call(s32[1]{0:T(128)} %bitcast.me_ref, f32[16,48,128]{2,1,0:T(8,128)S(1)} %all-to-all-done.block_ref, f32[256,128]{1,0:T(8,128)S(1)} %bitcast.8, f32[288,128]{1,0:T(8,128)S(1)} %collective-permute-done.low_ref, f32[288,128]{1,0:T(8,128)S(1)} %collective-permute-done.1.high_ref, ...), custom_call_target="tpu_custom_call" | custom-call | flops 268435456 | bytes 1048576 | tf_op jit(solution)/shard_map/third/pallas_call | solution.py:480
  43.6 4.3 %collective-permute-start.2 = (f32[12,128]{1,0:T(8,128)S(1)}, f32[12,128]{1,0:T(8,128)S(1)}, u32[]{:S(2)}, u32[]{:S(2)}) collective-permute-start(f32[12,128]{1,0:T(8,128)S(1)} %get-tuple-element.21), channel_id=1, source_target_pairs={{0,4},{1,5},{4,8},{5,9},{8,12},{9,13},{12,16},{13,17},{16,20},{17,... | collective-permute-start | bytes 18440 | tf_op jit(solution)/shard_map/ppermute | solution.py:489
  47.9 2.8 %window.1 = (f32[128,128]{1,0:T(8,128)S(1)}, f32[12,768,128]{2,1,0:T(8,128)S(1)}, f32[4,768,128]{2,1,0:T(8,128)S(1)}) custom-call(s32[1]{0:T(128)} %bitcast.me_ref, f32[16,48,128]{2,1,0:T(8,128)S(1)} %all-to-all-done.block_ref, f32[288,128]{1,0:T(8,128)S(1)} %collective-permute-done.low_ref, f32[288,128]{1,0:T(8,128)S(1)} %collective-permute-done.1.high_ref), custom_call_target="tpu_custom_call" | custom-call | flops 268435456 | bytes 1048576 | tf_op jit(solution)/shard_map/window/pallas_call | solution.py:490
  50.7 0.0 collective-permute-done.2.got_ref
  50.7 3.3 %fourth.1 = (f32[3,256]{1,0:T(4,128)}, f32[3,256]{1,0:T(4,128)}) custom-call(s32[1]{0:T(128)} %bitcast.me_ref, f32[128,128]{1,0:T(8,128)S(1)} %get-tuple-element.12.rows_ref, f32[12,768,128]{2,1,0:T(8,128)S(1)} %get-tuple-element.13.keep_ref, f32[4,768,128]{2,1,0:T(8,128)S(1)} %get-tuple-element.14.wide_ref, f32[24,128]{1,0:T(8,128)S(1)} %get-tuple-element.20.res_ref, ...), custom_call_target="tpu_custom_call" | custom-call | flops 268435456 | bytes 1048576 | tf_op jit(solution)/shard_map/fourth/pallas_call | solution.py:499
  (3 shorter events, 0.0 us)
Async XLA Ops:
  0.6 34.0 %copy-start = (f32[8,165,165]{2,0,1:T(8,128)S(1)}, f32[8,165,165]{2,0,1:T(8,128)}, u32[]{:S(2)}) copy-start(f32[8,165,165]{2,0,1:T(8,128)} %param.19) | copy-start | bytes 2613604
  0.6 0.8 %copy-start.1 = (f32[3,256]{1,0:T(4,128)S(1)}, f32[3,256]{1,0:T(4,128)}, u32[]{:S(2)}) copy-start(f32[3,256]{1,0:T(4,128)} %dip_ref.1) | copy-start | bytes 9220
  1.4 0.7 %copy-start.2 = (f32[3,256]{1,0:T(4,128)S(1)}, f32[3,256]{1,0:T(4,128)}, u32[]{:S(2)}) copy-start(f32[3,256]{1,0:T(4,128)} %perm_ref.1) | copy-start | bytes 9220
  2.1 0.7 %copy-start.3 = (f32[3,256]{1,0:T(4,128)S(1)}, f32[3,256]{1,0:T(4,128)}, u32[]{:S(2)}) copy-start(f32[3,256]{1,0:T(4,128)} %pos_ref.1) | copy-start | bytes 9220
  2.8 0.7 %copy-start.4 = (s32[2,189]{1,0:T(2,128)S(1)}, s32[2,189]{1,0:T(2,128)}, u32[]{:S(2)}) copy-start(s32[2,189]{1,0:T(2,128)} %boxes_ref.1) | copy-start | bytes 4540
  3.5 0.7 %copy-start.5 = (s32[2,189]{1,0:T(2,128)S(1)}, s32[2,189]{1,0:T(2,128)}, u32[]{:S(2)}) copy-start(s32[2,189]{1,0:T(2,128)} %class_ref.1) | copy-start | bytes 4540
  4.2 0.7 %copy-start.6 = (f32[2,189]{1,0:T(2,128)S(1)}, f32[2,189]{1,0:T(2,128)}, u32[]{:S(2)}) copy-start(f32[2,189]{1,0:T(2,128)} %scale_ref.1) | copy-start | bytes 4540
  4.9 0.7 %copy-start.7 = (f32[256]{0:T(256)S(1)}, f32[256]{0:T(256)}, u32[]{:S(2)}) copy-start(f32[256]{0:T(256)} %param.13) | copy-start | bytes 3076
  5.5 0.7 %copy-start.8 = (s32[2]{0:T(128)S(1)}, s32[2]{0:T(128)}, u32[]{:S(2)}) copy-start(s32[2]{0:T(128)} %occ_ref.1) | copy-start | bytes 28
  6.2 0.7 %copy-start.9 = (s32[2]{0:T(128)S(1)}, s32[2]{0:T(128)}, u32[]{:S(2)}) copy-start(s32[2]{0:T(128)} %count_ref.1) | copy-start | bytes 28
  8.6 17.1 %all-to-all-start = ((f32[16,48,128]{2,1,0:T(8,128)}), f32[16,48,128]{2,1,0:T(8,128)S(1)}, u32[]{:S(2)}, u32[]{:S(2)}) async-start(f32[16,48,128]{2,1,0:T(8,128)} %first.1), calls=%async_computation | async-start | bytes 786432 | tf_op jit(solution)/shard_map/all_to_all | solution.py:461
  27.6 12.4 %collective-permute-start.1 = (f32[288,128]{1,0:T(8,128)S(1)}, f32[288,128]{1,0:T(8,128)S(1)}, u32[]{:S(2)}, u32[]{:S(2)}) collective-permute-start(f32[288,128]{1,0:T(8,128)S(1)} %get-tuple-element.24), channel_id=1, source_target_pairs={{4,0},{5,1},{6,2},{7,3},{8,4},{9,5},{10,6},{11,7},{12,8},{13,9},{1... | collective-permute-start | bytes 442376 | tf_op jit(solution)/shard_map/ppermute | solution.py:470
  29.6 10.4 %collective-permute-start = (f32[288,128]{1,0:T(8,128)S(1)}, f32[288,128]{1,0:T(8,128)S(1)}, u32[]{:S(2)}, u32[]{:S(2)}) collective-permute-start(f32[288,128]{1,0:T(8,128)S(1)} %get-tuple-element.25), channel_id=1, source_target_pairs={{0,4},{1,5},{2,6},{3,7},{4,8},{5,9},{6,10},{7,11},{8,12},{9,13},{1... | collective-permute-start | bytes 442376 | tf_op jit(solution)/shard_map/ppermute | solution.py:469
  43.6 7.1 %collective-permute-start.2 = (f32[12,128]{1,0:T(8,128)S(1)}, f32[12,128]{1,0:T(8,128)S(1)}, u32[]{:S(2)}, u32[]{:S(2)}) collective-permute-start(f32[12,128]{1,0:T(8,128)S(1)} %get-tuple-element.21), channel_id=1, source_target_pairs={{0,4},{1,5},{4,8},{5,9},{8,12},{9,13},{12,16},{13,17},{16,20},{17,... | collective-permute-start | bytes 18440 | tf_op jit(solution)/shard_map/ppermute | solution.py:489

commit v3 on v2

--- a/solution.py
+++ b/solution.py
@@ -17,7 +17,7 @@
 NX = 4
 NY = 4
 PLANE = NX * NY
-CHUNK = 48
+CHUNK = 40
 F32 = jnp.float32
 BF16 = jnp.bfloat16
 
@@ -81,10 +81,20 @@
 
 
 def first_kernel(
-    me_ref, occ_ref, count_ref, dip_ref, perm_ref, pos_ref, pol_ref, boxes_ref, class_ref, scale_ref, out_ref, mono, chunk
+    me_ref, occ_ref, count_ref, dip_hbm, perm_hbm, pos_hbm, pol_hbm, boxes_hbm, class_hbm, scale_hbm, out_ref,
+    mono, chunk, dip_ref, perm_ref, pos_ref, pol_ref, scale_ref, boxes_ref, class_ref, sems,
 ):
+    pairs = (
+        (pos_hbm, pos_ref), (dip_hbm, dip_ref), (pol_hbm, pol_ref), (perm_hbm, perm_ref),
+        (boxes_hbm, boxes_ref), (class_hbm, class_ref), (scale_hbm, scale_ref),
+    )
+    copies = [pltpu.make_async_copy(source, target, sems.at[n]) for n, (source, target) in enumerate(pairs)]
+    for copy in copies:
+        copy.start()
     chunk[...] = jnp.zeros_like(chunk)
     lane = lax.broadcasted_iota(jnp.int32, (1, TILE), 1)
+    for copy in copies:
+        copy.wait()
     for w in range(2):
         live = (lane < occ_ref[w]).astype(F32)
         lanes = slice(w * TILE, (w + 1) * TILE)
@@ -108,9 +118,8 @@
     for w in range(2):
         weight = scale_ref[w : w + 1, :] * (entry < count_ref[w]).astype(F32)
         for n, row in enumerate((place[w : w + 1, :], kind[w : w + 1, :], weight)):
-            at = 32 + w * 6 + n * 2
-            chunk[at : at + 1, :] = row[:, :TILE]
-            chunk[at + 1 : at + 2, 0 : ILIST - TILE] = row[:, TILE:]
+            chunk[30 + w * 3 + n : 31 + w * 3 + n, :] = row[:, :TILE]
+            chunk[36 + n : 37 + n, w * 64 : w * 64 + ILIST - TILE] = row[:, TILE:]
     def both(row):
         two = chunk[pl.ds(8 + row, 2, stride=8), :]
         return jnp.concatenate([two, two, two, two], axis=0)
@@ -127,13 +136,6 @@
         out_ref[m, :, :] = whole
 
 
-def spread(wide_ref, cols, boxes, fields):
-    for slot, box in enumerate(boxes):
-        for f in fields:
-            at = box * 8 + f
-            wide_ref[f, slot * TILE : (slot + 1) * TILE, :] = jnp.broadcast_to(cols[:, at : at + 1], (TILE, TILE))
-
-
 def write_fields(rows_ref, number, px, py, pz, root, first_layer):
     box = lax.broadcasted_iota(jnp.int32, (number, TILE), 0)
     rows_ref[pl.ds(0, number, stride=8), :] = HALF * (px + 2.0 * (box & 1).astype(F32))
@@ -152,7 +154,7 @@
     inverse = lax.rsqrt(squared)
     inv_two = inverse * inverse
     inv_three = inverse * inv_two
-    minus = -((squared * (squared * inverse)) * roots)
+    minus = (squared * (squared * inverse)) * roots
     damping = jnp.exp(minus)
     lambda_three = 1.0 - damping
     lambda_five = lambda_three + minus * damping
@@ -183,17 +185,27 @@
     return ((count + 7.0) * 0.125).astype(jnp.int32)
 
 
-def near_box(total_ref, slot, wide_ref, target, trips, rows_ref, sources):
+def spread(wide_ref, cols, boxes, fields):
+    for slot, box in enumerate(boxes):
+        for f in fields:
+            at = box * 8 + f
+            value = jnp.broadcast_to(cols[:, at : at + 1], (TILE, TILE))
+            wide_ref[f, slot * TILE : (slot + 1) * TILE, :] = -value if f == 3 else value
+
+
+def near_boxes(total_ref, slots, wide_ref, targets, trips, rows_ref, sources):
     def body(n, carry):
-        at = tile_at(n, target * TILE)
-        mine = [wide_ref[f, at, :] for f in range(4)]
-        parts = []
+        mine = [[wide_ref[f, tile_at(n, target * TILE), :] for f in range(4)] for target in targets]
+        parts = [[] for _ in targets]
         for box in sources:
-            delta = [mine[c] - row(rows_ref, box * 8 + c) for c in range(3)]
-            radial, direct = scalars(delta, mine[3] * row(rows_ref, box * 8 + 3))
-            parts.append(field_of(delta, radial, direct, [row(rows_ref, box * 8 + 4 + c) for c in range(3)]))
-        for c in range(3):
-            total_ref[c, tile_at(n, slot * TILE), :] = added([part[c] for part in parts])
+            where = [row(rows_ref, box * 8 + f) for f in range(7)]
+            for i, spot in enumerate(mine):
+                delta = [spot[c] - where[c] for c in range(3)]
+                radial, direct = scalars(delta, spot[3] * where[3])
+                parts[i].append(field_of(delta, radial, direct, where[4:7]))
+        for i, slot in enumerate(slots):
+            for c in range(3):
+                total_ref[c, tile_at(n, slot * TILE), :] = added([part[c] for part in parts[i]])
         return carry
 
     lax.fori_loop(0, trips, body, 0)
@@ -216,7 +228,7 @@
         low_ref[o * 256 : o * 256 + NTERM, :] = low
 
 
-def second_kernel(me_ref, block_ref, sel_ref, near_ref, wide, rows, total):
+def second_kernel(me_ref, block_ref, sel_ref, near_ref, wide, m_high_ref, m_low_ref, rows, total, mono):
     mine = (me_ref[0] // (2 * OWNERS)) * NX
     rows[...] = jnp.zeros_like(rows)
     for x in range(NX):
@@ -227,43 +239,62 @@
 
     px, py, pz, root = field(0), field(1), field(2), root_of(field(3))
     trips = trips_of(field(7))
+    write_monomials(mono, px, py, pz)
     write_fields(rows, 8, px, py, pz, root, 0)
     spread(wide, jnp.transpose(rows[...]), range(8), range(4))
+    for k in range(8):
+        high, low = halves(mono[pl.ds(k, NTERM, stride=8), :])
+        m_high_ref[k * 176 : k * 176 + NTERM, :] = high
+        m_low_ref[k * 176 : k * 176 + NTERM, :] = low
     for box in range(8):
         low, high = max(box // 2 - 1, 0), min(box // 2 + 1, NX - 1)
-        near_box(total, box, wide, box, trips[box, 0], rows, range(low * 2, high * 2 + 2))
+        near_boxes(total, [box], wide, [box], trips[box, 0], rows, range(low * 2, high * 2 + 2))
     spot = lax.broadcasted_iota(jnp.int32, (192, TILE), 0)
     kinds = lax.broadcasted_iota(jnp.int32, (CLASSES, TILE), 0)
-    for k in range(8):
-        got = jnp.zeros((16, 192), F32)
-        for half in range(2):
-            at = 32 + (k % 2) * 6 + half
-            place = block_ref[mine + k // 2, at : at + 1, :].astype(jnp.int32)
-            kind = block_ref[mine + k // 2, at + 2 : at + 3, :].astype(jnp.int32)
-            weight = jnp.where(kinds == kind, block_ref[mine + k // 2, at + 4 : at + 5, :], 0.0)
+    side = lax.broadcasted_iota(jnp.int32, (CLASSES, TILE), 1) >> 6
+    for x in range(NX):
+        got = jnp.zeros((32, 192), F32)
+        first, second = [], []
+        for w in range(2):
+            at = 30 + w * 3
+            place = block_ref[mine + x, at : at + 1, :].astype(jnp.int32)
+            kind = block_ref[mine + x, at + 1 : at + 2, :].astype(jnp.int32)
+            weight = jnp.where(kinds == kind, block_ref[mine + x, at + 2 : at + 3, :], 0.0)
             chosen = jnp.where(spot == place, 1.0, 0.0).astype(BF16)
             high = weight.astype(BF16).astype(F32)
-            parts = jnp.concatenate([high, weight - high], axis=0).astype(BF16)
-            got = got + dot(parts, chosen, NT)
-        sel_ref[k * 8 : k * 8 + 8, :] = got[0:8] + got[8:16]
+            first.append(dot(jnp.concatenate([high, weight - high], axis=0).astype(BF16), chosen, NT))
+        place = block_ref[mine + x, 36:37, :].astype(jnp.int32)
+        kind = block_ref[mine + x, 37:38, :].astype(jnp.int32)
+        weight = jnp.where(kinds == kind, block_ref[mine + x, 38:39, :], 0.0)
+        high = weight.astype(BF16).astype(F32)
+        low = weight - high
+        both = [jnp.where(side == w, part, 0.0) for w in range(2) for part in (high, low)]
+        chosen = jnp.where(spot == place, 1.0, 0.0).astype(BF16)
+        second = dot(jnp.concatenate(both, axis=0).astype(BF16), chosen, NT)
+        for w in range(2):
+            k = x * 2 + w
+            tail = second[w * 16 : w * 16 + 16]
+            sel_ref[k * 8 : k * 8 + 8, :] = (first[w][0:8] + tail[0:8]) + (first[w][8:16] + tail[8:16])
     for c in range(3):
         for box in range(8):
             near_ref[c * 8 + box : c * 8 + box + 1, :] = lane_sums(total, c, box)
 
 
 def third_kernel(
-    me_ref, block_ref, own_ref, low_ref, high_ref, sel_ref, near_ref, wide_ref, t_high_ref, t_low_ref, res_ref, send_ref,
-    summed, local, mono, rows, total,
+    me_ref, block_ref, own_ref, sides_ref, sel_ref, near_ref, wide_ref, m_high_ref, m_low_ref, t_high_ref, t_low_ref,
+    res_ref, send_ref, summed, head, rest, far, rows, total,
 ):
     mine = (me_ref[0] // (2 * OWNERS)) * NX
+    core = lax.rem(me_ref[0] // OWNERS, 2)
     x_me = lax.rem(me_ref[0], NX)
     sel_high, sel_low = halves(sel_ref[...])
     both = jnp.concatenate([sel_high, sel_low], axis=0)
     for kind in range(4):
-        flat = jnp.concatenate(
-            [ref[pl.ds(kind * 2 + w, 32, stride=8), :] for w in range(2) for ref in (own_ref, low_ref, high_ref)], axis=0
-        )
-        high, low = halves(flat)
+        pieces = []
+        for w in range(2):
+            pieces += [own_ref[pl.ds(at + kind * 2 + w, 16, stride=8), :] for at in (0, OWN_ROWS)]
+            pieces += [sides_ref[pl.ds(at + kind * 2 + w, 32, stride=8), :] for at in (0, SIDE_ROWS)]
+        high, low = halves(jnp.concatenate(pieces, axis=0))
         got = dot(both, high, NN)
         summed[kind * 64 : kind * 64 + 64, :] = got[0:64] + (got[64:128] + dot(sel_high, low, NN))
     parts = []
@@ -271,18 +302,22 @@
         pieces = []
         for o in range(CLASSES):
             pieces.append(summed[pl.ds(c * 64 + o, 8, stride=8), :])
-            rest = summed[pl.ds(192 + o, 8, stride=8), :][:, c * REST : (c + 1) * REST]
-            pieces.append(jnp.concatenate([rest, jnp.zeros((8, TILE - REST), F32)], axis=1))
+            tail = summed[pl.ds(192 + o, 8, stride=8), :][:, c * REST : (c + 1) * REST]
+            pieces.append(jnp.concatenate([tail, jnp.zeros((8, TILE - REST), F32)], axis=1))
         parts.append(jnp.concatenate(pieces, axis=1))
+    parts.append(jnp.zeros((8, CLASSES * 256), F32))
     high, low = halves(jnp.concatenate(parts, axis=0))
-    t_high, t_low = t_high_ref[...], t_low_ref[...]
-    moved = dot(high, t_high, NN) + (dot(low, t_high, NN) + dot(high, t_low, NN))
-    local[:, 0:NTERM] = moved
+    got = dot(jnp.concatenate([high, low], axis=0), t_high_ref[...], NN)
+    moved = got[0:24] + (got[32:56] + dot(high, t_low_ref[...], NN)[0:24])
+    moved_high = moved.astype(BF16).astype(F32)
+    for n, part in enumerate((moved_high, moved - moved_high)):
+        head[n * 24 : n * 24 + 24, :] = part[:, 0:TILE]
+        rest[n * 24 : n * 24 + 24, 0:REST] = part[:, TILE:]
     rows[...] = jnp.zeros_like(rows)
-    rows[0:16, :] = low_ref[272:288, :]
+    rows[0:16, :] = sides_ref[pl.ds(pl.multiple_of(272 + 32 * core, 8), 16), :]
     for x in range(NX):
         rows[16 + x * 16 : 32 + x * 16, :] = block_ref[mine + x, 8:24, :]
-    rows[80:96, :] = high_ref[256:272, :]
+    rows[80:96, :] = sides_ref[pl.ds(pl.multiple_of(SIDE_ROWS + 256 + 32 * core, 8), 16), :]
 
     def field(f):
         return rows[pl.ds(f, 12, stride=8), :]
@@ -292,15 +327,18 @@
     source = [rows[pl.ds(16 + 4 + c, 8, stride=8), :] for c in range(3)]
     root = root_of(pol)
     trips = trips_of(live)
-    write_monomials(mono, px[2:10], py[2:10], pz[2:10])
     write_fields(rows, 12, px, py, pz, root, -1)
-    for slot, box, sources in ((0, 0, (0, 1)), (1, 1, (0, 1)), (2, 6, (10, 11)), (3, 7, (10, 11))):
-        near_box(total, slot, wide_ref, box, trips[box, 0], rows, sources)
-    far = [jnp.zeros((8, TILE), F32) for _ in range(3)]
-    for t in range(NTERM):
-        term = mono[t * 8 : t * 8 + 8, :]
+    for slots, boxes, sources in (((0, 1), (0, 1), (0, 1)), ((2, 3), (6, 7), (10, 11))):
+        most = jnp.maximum(trips[boxes[0], 0], trips[boxes[1], 0])
+        near_boxes(total, slots, wide_ref, boxes, most, rows, sources)
+    for k in range(8):
+        left = jnp.concatenate([head[pl.ds(k, 6, stride=8), :], rest[pl.ds(k, 6, stride=8), :][:, 0:REST]], axis=1)
+        left = left.astype(BF16)
+        with_high = dot(left, m_high_ref[k * 176 : k * 176 + NTERM, :], NN)
+        with_low = dot(left, m_low_ref[k * 176 : k * 176 + NTERM, :], NN)
+        value = with_high[0:3] + (with_high[3:6] + with_low[0:3])
         for c in range(3):
-            far[c] = far[c] + jnp.broadcast_to(local[c * 8 : c * 8 + 8, t : t + 1], (8, TILE)) * term
+            far[c * 8 + k : c * 8 + k + 1, :] = value[c : c + 1]
     alone = self_term(root[2:10])
     nothing = jnp.zeros((4, TILE), F32)
     for c in range(3):
@@ -311,7 +349,7 @@
         edge = jnp.concatenate(ends[0:2] + [nothing] + ends[2:4], axis=0)
         near_zero = near_ref[c * 8 : c * 8 + 8, :] + edge + alone * source[c]
         res_ref[c * 8 : c * 8 + 8, :] = jnp.where(
-            live > 0.0, perm + far[c] + near_zero - source[c] / pol[2:10], 0.0
+            live > 0.0, perm + far[c * 8 : c * 8 + 8, :] + near_zero - source[c] / pol[2:10], 0.0
         )
     first = jnp.where(x_me < 2, 4, 0)
     for c in range(3):
@@ -319,13 +357,14 @@
             send_ref[c * 4 + k : c * 4 + k + 1, :] = res_ref[pl.ds(c * 8 + first + k, 1), :]
 
 
-def window_kernel(me_ref, block_ref, low_ref, high_ref, rows, keep, wide, every):
+def window_kernel(me_ref, block_ref, sides_ref, rows, keep, wide, every):
     mine = (me_ref[0] // (2 * OWNERS)) * NX
+    core = lax.rem(me_ref[0] // OWNERS, 2)
     first = lax.rem(me_ref[0], NX) * 2
-    every[0:32, :] = low_ref[256:288, :]
+    every[0:32, :] = sides_ref[pl.ds(pl.multiple_of(256 + 32 * core, 8), 32), :]
     for x in range(NX):
         every[32 + x * 16 : 48 + x * 16, :] = block_ref[mine + x, 8:24, :]
-    every[96:128, :] = high_ref[256:288, :]
+    every[96:128, :] = sides_ref[pl.ds(pl.multiple_of(SIDE_ROWS + 256 + 32 * core, 8), 32), :]
     rows[...] = jnp.zeros_like(rows)
     for k in range(10):
         rows[k * 8 : k * 8 + 8, :] = every[pl.ds(pl.multiple_of((first + k) * 8, 8), 8), :]
@@ -409,6 +448,7 @@
 
 VMEM = pl.BlockSpec(memory_space=pltpu.VMEM)
 SMEM = pl.BlockSpec(memory_space=pltpu.SMEM)
+HBM = pl.BlockSpec(memory_space=pltpu.HBM)
 
 
 def shape_of(shape):
@@ -421,7 +461,7 @@
         in_specs=ins,
         out_specs=[VMEM] * len(outs),
         out_shape=[shape_of(shape) for shape in outs],
-        scratch_shapes=[pltpu.VMEM(shape, F32) for shape in scratch],
+        scratch_shapes=[pltpu.VMEM(shape, F32) if isinstance(shape, tuple) else shape for shape in scratch],
         cost_estimate=pl.CostEstimate(flops=cost, bytes_accessed=1 << 20, transcendentals=0),
         compiler_params=pltpu.CompilerParams(vmem_limit_bytes=limit << 20),
         name=name,
@@ -439,21 +479,34 @@
         for z in range(OWNERS // NX)
     ]
     chip = [[device(2 * y, b), device(2 * y + 1, b)] for y in range(NY) for b in range(OWNERS)]
-    up = [(device(g, b), device(g, b + NX)) for g in range(GROUPS) for b in range(OWNERS - NX)]
-    down = [(target, source) for source, target in up]
-    near_side = [(s, t) for s, t in up if s % NX < 2] + [(s, t) for s, t in down if s % NX >= 2]
-    return plane, chip, up, down, near_side
-
-
-PLANE_SETS, CHIP_SETS, UP, DOWN, NEAR_SIDE = rounds()
+    up = [[(device(g, b), device(g, b + NX)) for b in range(OWNERS - NX)] for g in range(GROUPS)]
+    down = [[(target, source) for source, target in pairs] for pairs in up]
+    apart = [pair for g in range(GROUPS) for pair in (down[g] if g % 2 else up[g])]
+    near_side = [(s, t) for pairs in up for s, t in pairs if s % NX < 2]
+    near_side += [(s, t) for pairs in down for s, t in pairs if s % NX >= 2]
+    return plane, chip, apart, near_side
+
+
+PLANE_SETS, CHIP_SETS, APART, NEAR_SIDE = rounds()
+OWN_ROWS = PLANE * 8 + 64
+SIDE_ROWS = 256 + 64
 
 
 def on_device(
     dipoles, perm_field, positions, polarizability, occupancy, far_boxes, far_class, far_count, far_scale, translations
 ):
     me = lax.axis_index("d").astype(jnp.int32)[None]
+    lists = pltpu.VMEM((2, ILIST), jnp.int32)
     [chunk] = call(
-        first_kernel, [SMEM] * 3 + [VMEM] * 7, [(PLANE, CHUNK, TILE)], [(NTERM * 8, TILE), (CHUNK, TILE)], 1 << 20, 8, "first"
+        first_kernel,
+        [SMEM] * 3 + [HBM] * 7,
+        [(PLANE, CHUNK, TILE)],
+        [(NTERM * 8, TILE), (CHUNK, TILE)]
+        + [(3, 2 * TILE)] * 3
+        + [(1, 2 * TILE), (2, ILIST), lists, lists, pltpu.SemaphoreType.DMA((7,))],
+        1 << 20,
+        60,
+        "first",
     )(
         me, occupancy, far_count, dipoles, perm_field, positions, polarizability.reshape(1, 2 * TILE),
         far_boxes, far_class, far_scale,
@@ -463,39 +516,47 @@
     t_high, t_low = call(prepare_kernel, [VMEM], [half, half], [], 1 << 28, 12, "prepare")(
         jnp.transpose(translations, (1, 0, 2))
     )
-    own = lax.all_gather(block[:, 0:8, :], "d", axis_index_groups=CHIP_SETS, axis=0).reshape(256, TILE)
     mine = (me[0] // (2 * OWNERS)) * NX
-    near = lax.dynamic_slice(block, (mine, 8, 0), (NX, 16, TILE))
-    low = lax.ppermute(jnp.concatenate([own, near[2:4].reshape(32, TILE)], axis=0), "d", UP)
-    high = lax.ppermute(jnp.concatenate([own, near[0:2].reshape(32, TILE)], axis=0), "d", DOWN)
-    sel, near_zero, wide = call(
+    core = (me[0] // OWNERS) % 2
+    near = lax.dynamic_slice(block, (mine, 8, 0), (NX, 16, TILE)).reshape(64, TILE)
+    part = jnp.concatenate([block[:, 0:8, :].reshape(PLANE * 8, TILE), near], axis=0)
+    part, t_high, t_low = lax.optimization_barrier((part, t_high, t_low))
+    own = lax.all_gather(part, "d", axis_index_groups=CHIP_SETS, axis=0)
+    edges = lax.dynamic_slice(own, (0, PLANE * 8 + 32 * (1 - core), 0), (2, 32, TILE)).reshape(64, TILE)
+    away = jnp.concatenate([own[:, 0 : PLANE * 8].reshape(256, TILE), edges], axis=0)
+    came = lax.ppermute(away, "d", APART)
+    own = own.reshape(2 * OWN_ROWS, TILE)
+    half = jax.ShapeDtypeStruct((8 * 176, TILE), BF16)
+    sel, near_zero, wide, m_high, m_low = call(
         second_kernel,
         [SMEM, VMEM],
-        [(64, 192), (24, TILE), (4, 8 * TILE, TILE)],
-        [(TILE, TILE), (3, 8 * TILE, TILE)],
+        [(64, 192), (24, TILE), (4, 8 * TILE, TILE), half, half],
+        [(TILE, TILE), (3, 8 * TILE, TILE), (NTERM * 8, TILE)],
         1 << 28,
         12,
         "second",
     )(me, block)
+    came, sel = lax.optimization_barrier((came, sel))
+    sides = lax.all_gather(came, "d", axis_index_groups=CHIP_SETS, axis=0).reshape(2 * SIDE_ROWS, TILE)
     residual, send = call(
         third_kernel,
-        [SMEM] + [VMEM] * 9,
+        [SMEM] + [VMEM] * 10,
         [(24, TILE), (12, TILE)],
-        [(256, TILE), (24, 256), (NTERM * 8, TILE), (TILE, TILE), (3, 4 * TILE, TILE)],
+        [(256, TILE), (48, TILE), (48, TILE), (24, TILE), (TILE, TILE), (3, 4 * TILE, TILE)],
         1 << 28,
         16,
         "third",
-    )(me, block, own, low, high, sel, near_zero, wide, t_high, t_low)
+    )(me, block, own, sides, sel, near_zero, wide, m_high, m_low, t_high, t_low)
     got = lax.ppermute(send, "d", NEAR_SIDE)
-    rows, keep, spread_out = call(
+    rows, keep, wide = call(
         window_kernel,
-        [SMEM] + [VMEM] * 3,
+        [SMEM] + [VMEM] * 2,
         [(TILE, TILE), (12, 6 * TILE, TILE), (4, 6 * TILE, TILE)],
         [(TILE, TILE)],
         1 << 28,
         16,
         "window",
-    )(me, block, low, high)
+    )(me, block, sides)
     new, out = call(
         fourth_kernel,
         [SMEM] + [VMEM] * 5,
@@ -504,7 +565,7 @@
         1 << 28,
         16,
         "fourth",
-    )(me, rows, keep, spread_out, residual, got)
+    )(me, rows, keep, wide, residual, got)
     return new, out
 
 

time: 55 us -> 46.9 us (0.85)
  the two profiles are of different devices: /device:TPU:224 before, /device:TPU:225 now
where the time goes in v3:
time: 46.9 us; the launch traced here: 46.2 us
  Pallas kernels  17.1 us (36%)
  starting transfers between devices  12.4 us (26%)
  blocking collectives  7.4 us (16%)
  waiting for transfers between devices  7.15 us (15%)
  local copies, waits for them, and re-layouts  1.36 us (3%)
  between operations  0.78 us (2%)
    all_to_all x1, starting transfers between devices, on_device(): lax.all_to_all(chunk, 'd', 0, 0, axis_index_groups=PLANE_SETS, tiled=True)  6.77 us
    all_to_all x1, waiting for transfers between devices, on_device(): lax.all_to_all(chunk, 'd', 0, 0, axis_index_groups=PLANE_SETS, tiled=True)  6.38 us
    pallas_call x1, Pallas kernels, on_device(): call(second_kernel, [SMEM, VMEM], [(64, 192), (24, TILE), (4, 8 * TILE, T...  4.76 us
    all_gather x1, blocking collectives, on_device(): lax.all_gather(came, 'd', axis_index_groups=CHIP_SETS, axis=0)  4 us
    ppermute x1, starting transfers between devices, on_device(): got = lax.ppermute(send, 'd', NEAR_SIDE)  3.74 us
    all_gather x1, blocking collectives, on_device(): own = lax.all_gather(part, 'd', axis_index_groups=CHIP_SETS, axis=0)  3.4 us
    pallas_call x1, Pallas kernels, on_device(): call(fourth_kernel, [SMEM] + [VMEM] * 5, [(3, 2 * TILE), (3, 2 * TILE)],...  3.33 us
    pallas_call x1, Pallas kernels, on_device(): call(window_kernel, [SMEM] + [VMEM] * 2, [(TILE, TILE), (12, 6 * TILE, TI...  2.87 us
  transfers between devices with their start and end apart: 3, of which 2 were waited for; matrix products, arithmetic and copies ran while one was open for 0% of the time, Pallas kernels for 18%

profile of v3, /device:TPU:225, one launch (start us, length us, event | category | flops | bytes accessed | tf_op | source)
XLA Modules:
  0.0 46.2 jit_solution(9363372331234767048)
XLA Ops:
  0.6 2.6 %first.1 = f32[16,40,128]{2,1,0:T(8,128)} custom-call(s32[1]{0:T(128)} %bitcast.me_ref, s32[2]{0:T(128)} %occ_ref.1, s32[2]{0:T(128)} %count_ref.1, f32[3,256]{1,0:T(4,128)} %dip_hbm.1, f32[3,256]{1,0:T(4,128)} %perm_hbm.1, f32[3,256]{1,0:T(4,128)} %pos_hbm.1, f32[1,256]{1,0:T(1,128)} %bitcast.15, s32[2,189]{1,0:T(2,128)} %boxes_hbm.1, s32[2,189]{1,0:T(2,128)} %class_hbm.1, ...), custom_call_target="tpu_custom_call" | custom-call | flops 1048576 | bytes 1048576 | tf_op jit(solution)/shard_map/first/pallas_call | solution.py:500
  3.3 6.8 %all-to-all-start = ((f32[16,40,128]{2,1,0:T(8,128)}), f32[16,40,128]{2,1,0:T(8,128)S(1)}, u32[]{:S(2)}, u32[]{:S(2)}) async-start(f32[16,40,128]{2,1,0:T(8,128)} %first.1), calls=%async_computation | async-start | bytes 655360 | tf_op jit(solution)/shard_map/all_to_all | solution.py:514
  10.1 0.0 copy-start
  10.1 1.3 %copy-done = f32[8,165,165]{2,0,1:T(8,128)S(1)} copy-done((f32[8,165,165]{2,0,1:T(8,128)S(1)}, f32[8,165,165]{2,0,1:T(8,128)}, u32[]{:S(2)}) %copy-start) | copy-done | bytes 871224
  11.4 0.8 %prepare.1 = (bf16[2048,165]{1,0:T(8,128)(2,1)S(1)}, bf16[2048,165]{1,0:T(8,128)(2,1)S(1)}) custom-call(f32[165,8,165]{2,1,0:T(8,128)S(1)} %bitcast.11), custom_call_target="tpu_custom_call" | custom-call | flops 268435456 | bytes 1048576 | tf_op jit(solution)/shard_map/prepare/pallas_call | solution.py:516
  12.2 6.4 %all-to-all-done.block_ref = f32[16,40,128]{2,1,0:T(8,128)S(1)} async-done(((f32[16,40,128]{2,1,0:T(8,128)}), f32[16,40,128]{2,1,0:T(8,128)S(1)}, u32[]{:S(2)}, u32[]{:S(2)}) %all-to-all-start) | async-done | bytes 327712 | tf_op jit(solution)/shard_map/all_to_all | solution.py:514
  18.6 3.4 %all-gather.own_ref = f32[384,128]{1,0:T(8,128)S(1)} all-gather(f32[192,128]{1,0:T(8,128)S(1)} %pad_maximum_fusion.1), channel_id=2, replica_groups={{0,64},{1,65},{2,66},{3,67},{4,68},{5,69},{6,70},{7,71},{8,72},{9,73},{..., dimensions={0}, use_global_device_ids=true | all-gather | bytes 294912 | tf_op jit(solution)/shard_map/all_gather | solution.py:524
  22.1 1.9 %collective-permute-start = (f32[320,128]{1,0:T(8,128)S(1)}, f32[320,128]{1,0:T(8,128)S(1)}, u32[]{:S(2)}, u32[]{:S(2)}) collective-permute-start(f32[320,128]{1,0:T(8,128)S(1)} %pad_maximum_fusion), channel_id=1, source_target_pairs={{0,4},{1,5},{2,6},{3,7},{4,8},{5,9},{6,10},{7,11},{8,12},{9,13},{1... | collective-permute-start | bytes 491528 | tf_op jit(solution)/shard_map/ppermute | solution.py:527
  24.0 4.8 %second.1 = (f32[64,192]{1,0:T(8,128)S(1)}, f32[24,128]{1,0:T(8,128)S(1)}, f32[4,1024,128]{2,1,0:T(8,128)S(1)}, bf16[1408,128]{1,0:T(8,128)(2,1)S(1)}, bf16[1408,128]{1,0:T(8,128)(2,1)S(1)}) custom-call(s32[1]{0:T(128)} %bitcast.me_ref, f32[16,40,128]{2,1,0:T(8,128)S(1)} %all-to-all-done.block_ref), custom_call_target="tpu_custom_call" | custom-call | flops 268435456 | bytes 1048576 | tf_op jit(solution)/shard_map/second/pallas_call | solution.py:530
  28.8 0.8 %collective-permute-done = f32[320,128]{1,0:T(8,128)S(1)} collective-permute-done((f32[320,128]{1,0:T(8,128)S(1)}, f32[320,128]{1,0:T(8,128)S(1)}, u32[]{:S(2)}, u32[]{:S(2)}) %collective-permute-start) | collective-permute-done | bytes 163872 | tf_op jit(solution)/shard_map/ppermute | solution.py:527
  29.5 4.0 %all-gather.1.sides_ref = f32[640,128]{1,0:T(8,128)S(1)} all-gather(f32[320,128]{1,0:T(8,128)S(1)} %collective-permute-done), channel_id=3, replica_groups={{0,64},{1,65},{2,66},{3,67},{4,68},{5,69},{6,70},{7,71},{8,72},{9,73},{..., dimensions={0}, use_global_device_ids=true | all-gather | bytes 491520 | tf_op jit(solution)/shard_map/all_gather | solution.py:540
  33.5 2.8 %third.1 = (f32[24,128]{1,0:T(8,128)S(1)}, f32[12,128]{1,0:T(8,128)S(1)}) custom-call(s32[1]{0:T(128)} %bitcast.me_ref, f32[16,40,128]{2,1,0:T(8,128)S(1)} %all-to-all-done.block_ref, f32[384,128]{1,0:T(8,128)S(1)} %all-gather.own_ref, f32[640,128]{1,0:T(8,128)S(1)} %all-gather.1.sides_ref, f32[64,192]{1,0:T(8,128)S(1)} %get-tuple-element.27.sel_ref, ...), custom_call_target="tpu_custom_call" | custom-call | flops 268435456 | bytes 1048576 | tf_op jit(solution)/shard_map/third/pallas_call | solution.py:541
  36.3 3.7 %collective-permute-start.1 = (f32[12,128]{1,0:T(8,128)S(1)}, f32[12,128]{1,0:T(8,128)S(1)}, u32[]{:S(2)}, u32[]{:S(2)}) collective-permute-start(f32[12,128]{1,0:T(8,128)S(1)} %get-tuple-element.35), channel_id=1, source_target_pairs={{0,4},{1,5},{4,8},{5,9},{8,12},{9,13},{12,16},{13,17},{16,20},{17,... | collective-permute-start | bytes 18440 | tf_op jit(solution)/shard_map/ppermute | solution.py:550
  40.0 2.9 %window.1 = (f32[128,128]{1,0:T(8,128)S(1)}, f32[12,768,128]{2,1,0:T(8,128)S(1)}, f32[4,768,128]{2,1,0:T(8,128)S(1)}) custom-call(s32[1]{0:T(128)} %bitcast.me_ref, f32[16,40,128]{2,1,0:T(8,128)S(1)} %all-to-all-done.block_ref, f32[640,128]{1,0:T(8,128)S(1)} %all-gather.1.sides_ref), custom_call_target="tpu_custom_call" | custom-call | flops 268435456 | bytes 1048576 | tf_op jit(solution)/shard_map/window/pallas_call | solution.py:551
  42.9 0.0 collective-permute-done.1.got_ref
  42.9 3.3 %fourth.1 = (f32[3,256]{1,0:T(4,128)}, f32[3,256]{1,0:T(4,128)}) custom-call(s32[1]{0:T(128)} %bitcast.me_ref, f32[128,128]{1,0:T(8,128)S(1)} %get-tuple-element.24.rows_ref, f32[12,768,128]{2,1,0:T(8,128)S(1)} %get-tuple-element.25.keep_ref, f32[4,768,128]{2,1,0:T(8,128)S(1)} %get-tuple-element.26.wide_ref, f32[24,128]{1,0:T(8,128)S(1)} %get-tuple-element.34.res_ref, ...), custom_call_target="tpu_custom_call" | custom-call | flops 268435456 | bytes 1048576 | tf_op jit(solution)/shard_map/fourth/pallas_call | solution.py:560
  (6 shorter events, 0.1 us)
Async XLA Ops:
  3.3 15.3 %all-to-all-start = ((f32[16,40,128]{2,1,0:T(8,128)}), f32[16,40,128]{2,1,0:T(8,128)S(1)}, u32[]{:S(2)}, u32[]{:S(2)}) async-start(f32[16,40,128]{2,1,0:T(8,128)} %first.1), calls=%async_computation | async-start | bytes 655360 | tf_op jit(solution)/shard_map/all_to_all | solution.py:514
  10.1 1.3 %copy-start = (f32[8,165,165]{2,0,1:T(8,128)S(1)}, f32[8,165,165]{2,0,1:T(8,128)}, u32[]{:S(2)}) copy-start(f32[8,165,165]{2,0,1:T(8,128)} %param.19) | copy-start | bytes 2613604
  22.1 7.5 %collective-permute-start = (f32[320,128]{1,0:T(8,128)S(1)}, f32[320,128]{1,0:T(8,128)S(1)}, u32[]{:S(2)}, u32[]{:S(2)}) collective-permute-start(f32[320,128]{1,0:T(8,128)S(1)} %pad_maximum_fusion), channel_id=1, source_target_pairs={{0,4},{1,5},{2,6},{3,7},{4,8},{5,9},{6,10},{7,11},{8,12},{9,13},{1... | collective-permute-start | bytes 491528 | tf_op jit(solution)/shard_map/ppermute | solution.py:527
  36.3 6.6 %collective-permute-start.1 = (f32[12,128]{1,0:T(8,128)S(1)}, f32[12,128]{1,0:T(8,128)S(1)}, u32[]{:S(2)}, u32[]{:S(2)}) collective-permute-start(f32[12,128]{1,0:T(8,128)S(1)} %get-tuple-element.35), channel_id=1, source_target_pairs={{0,4},{1,5},{4,8},{5,9},{8,12},{9,13},{12,16},{13,17},{16,20},{17,... | collective-permute-start | bytes 18440 | tf_op jit(solution)/shard_map/ppermute | solution.py:550
